TPU v7x, 128 devices: a whole 4x4x4 slice. The times are simulated.
128 devices in a mesh: shot: 4 (over z_hi, core), gx: 16 (over x, y), gy: 2 (over z_lo).
Axes of the slice: x: 4, y: 4, z: 4 (z_hi: 2, z_lo: 2; z = z_hi * 2 + z_lo), core: 2. Of those that a mesh axis runs over, the one named last changes fastest.
Arguments:
- wave_now: float32 [4, 4, 512, 64, 128], P('shot', None, 'gx', 'gy'), may hold values from -6 to 6
- wave_prev: float32 [4, 4, 512, 64, 128], P('shot', None, 'gx', 'gy'), may hold values from -6 to 6
- vel_coef: float32 [512, 64, 128], P('gx', 'gy'), may hold values from 0.08 to 0.18
- epsilon: float32 [512, 64, 128], P('gx', 'gy'), may hold values from 0.15 to 0.35
- delta: float32 [512, 64, 128], P('gx', 'gy'), may hold values from 0 to 0.15
- tilt: int32 [512, 64, 128], P('gx', 'gy'), may hold values from 0 to 60
- azimuth: int32 [512, 64, 128], P('gx', 'gy'), may hold values from 0 to 359
- aperture: int32 [4, 16, 2], P('shot', 'gx', 'gy'), may hold values 0 or 1
Outputs:
- wave_final: float32 [4, 4, 512, 64, 128], P('shot', None, 'gx', 'gy')
- image: float32 [512, 64, 128], P('gx', 'gy')
All inputs are finite; a program needn't handle non-finite values. No bound on the sum of `aperture` on one device may be relied on, other than what follows from the above.
Results may differ from a plain program's by a relative error of at most 0.00002.
Values sent between devices are 32-bit elements; how exact they have to be, the bound alone decides.
A program may use at most 128 MiB of HBM per device.

v0:
```python
import math

import jax
import jax.numpy as jnp
from jax import lax
from jax.sharding import PartitionSpec as P

ITERS = 4


def extended(block, sides, width):
    for axis, dim in sides:
        count = lax.axis_size(axis)
        forward = [(i, i + 1) for i in range(count - 1)]
        backward = [(target, source) for source, target in forward]
        low = lax.ppermute(
            lax.slice_in_dim(block, block.shape[dim] - width, None, axis=dim), axis, forward
        )
        high = lax.ppermute(lax.slice_in_dim(block, 0, width, axis=dim), axis, backward)
        block = jnp.concatenate([low, block, high], axis=dim)
    return block


def model_terms(vel_coef, epsilon, delta, tilt, azimuth):
    theta = tilt.astype(jnp.float32) * (math.pi / 180.0)
    phi = azimuth.astype(jnp.float32) * (math.pi / 180.0)
    normal_x = jnp.sin(theta) * jnp.cos(phi)
    normal_y = jnp.sin(theta) * jnp.sin(phi)
    normal_z = jnp.cos(theta)
    gain = 1.0 + 2.0 * epsilon
    root = jnp.sqrt(1.0 + 2.0 * delta)
    return jnp.stack([normal_x, normal_y, normal_z, vel_coef, gain, root], axis=0)


def advance(padded, previous, coef):
    width_x = padded.shape[-3] - 2
    width_y = padded.shape[-2] - 2
    width_z = padded.shape[-1] - 2

    def shifted(off_x, off_y, off_z):
        return padded[
            ...,
            1 + off_x : 1 + off_x + width_x,
            1 + off_y : 1 + off_y + width_y,
            1 + off_z : 1 + off_z + width_z,
        ]

    centre = shifted(0, 0, 0)
    second_x = shifted(1, 0, 0) + shifted(-1, 0, 0) - 2.0 * centre
    second_y = shifted(0, 1, 0) + shifted(0, -1, 0) - 2.0 * centre
    second_z = shifted(0, 0, 1) + shifted(0, 0, -1) - 2.0 * centre
    mixed_xy = 0.25 * (
        shifted(1, 1, 0) - shifted(1, -1, 0) - shifted(-1, 1, 0) + shifted(-1, -1, 0)
    )
    mixed_xz = 0.25 * (
        shifted(1, 0, 1) - shifted(1, 0, -1) - shifted(-1, 0, 1) + shifted(-1, 0, -1)
    )
    mixed_yz = 0.25 * (
        shifted(0, 1, 1) - shifted(0, 1, -1) - shifted(0, -1, 1) + shifted(0, -1, -1)
    )
    normal_x, normal_y, normal_z = (coef[0], coef[1], coef[2])
    speed, gain, root = (coef[3], coef[4], coef[5])
    along = (
        normal_x * normal_x * second_x
        + normal_y * normal_y * second_y
        + normal_z * normal_z * second_z
        + 2.0
        * (
            normal_x * normal_y * mixed_xy
            + normal_x * normal_z * mixed_xz
            + normal_y * normal_z * mixed_yz
        )
    )
    across = second_x + second_y + second_z - along
    pressure = centre[:, 0::2]
    auxiliary = centre[:, 1::2]
    rhs_p = gain * across[:, 0::2] + root * along[:, 1::2]
    rhs_q = root * across[:, 0::2] + along[:, 1::2]
    next_p = 2.0 * pressure - previous[:, 0::2] + speed * rhs_p
    next_q = 2.0 * auxiliary - previous[:, 1::2] + speed * rhs_q
    return jnp.stack([next_p, next_q], axis=2).reshape(centre.shape)


def depth_pad(array):
    return jnp.pad(array, ((0, 0), (0, 0), (0, 0), (0, 0), (1, 1)))


def local(wave_now, wave_prev, vel_coef, epsilon, delta, tilt, azimuth, aperture):
    coef = model_terms(vel_coef, epsilon, delta, tilt, azimuth)
    correlation = jnp.zeros(vel_coef.shape, jnp.float32)
    current, previous = (wave_now, wave_prev)
    for step in range(ITERS):
        widened_now = extended(current, (("gx", 2), ("gy", 3)), 1)
        fresh = advance(depth_pad(widened_now), previous, coef)
        correlation = correlation + fresh[0, 0] * fresh[0, 2]
        previous, current = (current, fresh)
    covered = aperture[0, 0, 0].astype(jnp.float32)
    image = lax.psum(covered * correlation, "shot") / ITERS
    return (current, image)


def solution(mesh):
    return jax.shard_map(
        local,
        mesh=mesh,
        in_specs=(
            P("shot", None, "gx", "gy", None),
            P("shot", None, "gx", "gy", None),
            P("gx", "gy", None),
            P("gx", "gy", None),
            P("gx", "gy", None),
            P("gx", "gy", None),
            P("gx", "gy", None),
            P("shot", "gx", "gy"),
        ),
        out_specs=(P("shot", None, "gx", "gy", None), P("gx", "gy", None)),
        check_vma=False,
    )
```

profile of v0, /device:TPU:7, one launch (start us, length us, event | category | flops | bytes accessed | tf_op | source)
XLA Modules:
  0.0 221.6 jit_solution(3460875306081777361)
XLA Ops:
  7.2 0.9 fusion.71
  8.1 3.2 %collective-permute-start.1 = (f32[1,4,1,32,128]{4,3,2,1,0:T(8,128)S(1)}, f32[1,4,1,32,128]{4,3,2,1,0:T(8,128)S(1)}, u32[]{:S(2)}, u32[]{:S(2)}) collective-permute-start(f32[1,4,1,32,128]{4,3,2,1,0:T(8,128)S(1)} %get-tuple-element.39), channel_id=1, source_target_pairs={{0,2},{2,4},{4,6},{6,8},{8,10},{10,12},{12,14},{14,16},{16,18},{18... | collective-permute-start | bytes 196616 | tf_op jit(solution)/shard_map/ppermute | solution.py:16
  11.3 4.3 %collective-permute-start = (f32[1,4,1,32,128]{4,3,2,1,0:T(8,128)S(1)}, f32[1,4,1,32,128]{4,3,2,1,0:T(8,128)S(1)}, u32[]{:S(2)}, u32[]{:S(2)}) collective-permute-start(f32[1,4,1,32,128]{4,3,2,1,0:T(8,128)S(1)} %get-tuple-element.38), channel_id=1, source_target_pairs={{2,0},{4,2},{6,4},{8,6},{10,8},{12,10},{14,12},{16,14},{18,16},{20... | collective-permute-start | bytes 196616 | tf_op jit(solution)/shard_map/ppermute | solution.py:19
  15.7 6.1 %fusion.61 = (f32[32,32,128]{2,1,0:T(8,128)S(1)}, f32[32,32,128]{2,1,0:T(8,128)S(1)}, f32[32,32,128]{2,1,0:T(8,128)S(1)}, f32[32,32,128]{2,1,0:T(8,128)S(1)}, f3...) fusion(s32[32,32,128]{2,1,0:T(8,128)} %param.14, s32[32,32,128]{2,1,0:T(8,128)} %param.13), kind=kLoop, calls=%fused_computation.183 | loop fusion | flops 1966080 | bytes 4194304 | tf_op jit(solution)/shard_map/mul | solution.py:64
  21.8 0.2 constant_dynamic-update-slice_fusion.1
  22.2 1.4 collective-permute-start.2
  23.6 4.0 %collective-permute-start.3 = (f32[1,4,34,1,128]{4,3,2,1,0:T(1,128)S(1)}, f32[1,4,34,1,128]{4,3,2,1,0:T(1,128)S(1)}, u32[]{:S(2)}, u32[]{:S(2)}) collective-permute-start(f32[1,4,34,1,128]{4,3,2,1,0:T(1,128)S(1)} %get-tuple-element.30), channel_id=1, source_target_pairs={{0,1},{2,3},{4,5},{6,7},{8,9},{10,11},{12,13},{14,15},{16,17},{18,... | collective-permute-start | bytes 208904 | tf_op jit(solution)/shard_map/ppermute | solution.py:16
  27.7 0.2 add_sqrt_fusion
  27.9 1.1 collective-permute-done.3
  29.0 2.7 %select_maximum_fusion.12 = f32[1,4,34,34,130]{4,3,2,1,0:T(8,128)S(1)} fusion(f32[1,4,34,1,128]{4,3,2,1,0:T(1,128)S(1)} %collective-permute-done.2, f32[1,4,34,32,128]{4,3,2,1,0:T(8,128)S(1)} %constant_dynamic-update-slice_fusion, f32[1,4,34,1,128]{4,3,2,1,0:T(1,128)S(1)} %collective-permute-done.3), kind=kLoop, calls=%fused_computation.14 | loop fusion | flops 4808960 | bytes 4771968 | tf_op jit(solution)/shard_map/concatenate | solution.py:20
  31.8 8.4 %add_subtract_fusion.3 = (f32[1,4,32,32,128]{4,3,2,1,0:T(8,128)S(1)}, f32[1,4,32,32,128]{4,3,2,1,0:T(8,128)S(1)}) fusion(f32[1,4,32,32,128]{4,3,2,1,0:T(8,128)S(1)} %copy-done.2, f32[1,4,1,32,128]{4,3,2,1,0:T(8,128)S(1)} %collective-permute-done.1, f32[1,4,1,32,128]{4,3,2,1,0:T(8,128)S(1)} %collective-permute-done, ...), kind=kLoop, calls=%fused_computation.140 | loop fusion | flops 22544384 | bytes 32907264 | tf_op jit(solution)/shard_map/sub | solution.py:74
  40.3 2.5 %add_bitcast_fusion.7 = (f32[1,2,1,32,32,128]{5,4,3,1,2,0:T(8,128)S(1)}, f32[1,2,1,32,32,128]{5,4,3,1,2,0:T(8,128)S(1)}) fusion(f32[1,4,32,32,128]{4,3,2,1,0:T(8,128)} %param.9, f32[1,4,32,32,128]{4,3,2,1,0:T(8,128)S(1)} %get-tuple-element.9, f32[1,4,32,32,128]{4,3,2,1,0:T(8,128)S(1)} %get-tuple-element.8, f32[1,4,32,32,128]{4,3,2,1,0:T(8,128)S(1)} %copy-done.2, ...), kind=kLoop, calls=%fused_computation.148 | loop fusion | flops 3407872 | bytes 9961472 | tf_op jit(solution)/shard_map/stack | solution.py:81
  42.8 0.2 pad_maximum_fusion.13
  43.2 2.8 %collective-permute-start.4 = (f32[1,4,1,32,128]{4,3,2,1,0:T(8,128)S(1)}, f32[1,4,1,32,128]{4,3,2,1,0:T(8,128)S(1)}, u32[]{:S(2)}, u32[]{:S(2)}) collective-permute-start(f32[1,4,1,32,128]{4,3,2,1,0:T(8,128)S(1)} %get-tuple-element.36), channel_id=1, source_target_pairs={{2,0},{4,2},{6,4},{8,6},{10,8},{12,10},{14,12},{16,14},{18,16},{20... | collective-permute-start | bytes 196616 | tf_op jit(solution)/shard_map/ppermute | solution.py:19
  46.0 2.5 %collective-permute-start.5 = (f32[1,4,1,32,128]{4,3,2,1,0:T(8,128)S(1)}, f32[1,4,1,32,128]{4,3,2,1,0:T(8,128)S(1)}, u32[]{:S(2)}, u32[]{:S(2)}) collective-permute-start(f32[1,4,1,32,128]{4,3,2,1,0:T(8,128)S(1)} %get-tuple-element.37), channel_id=1, source_target_pairs={{0,2},{2,4},{4,6},{6,8},{8,10},{10,12},{12,14},{14,16},{16,18},{18... | collective-permute-start | bytes 196616 | tf_op jit(solution)/shard_map/ppermute | solution.py:16
  48.6 4.6 %collective-permute-done.5 = f32[1,4,1,32,128]{4,3,2,1,0:T(8,128)S(1)} collective-permute-done((f32[1,4,1,32,128]{4,3,2,1,0:T(8,128)S(1)}, f32[1,4,1,32,128]{4,3,2,1,0:T(8,128)S(1)}, u32[]{:S(2)}, u32[]{:S(2)}) %collective-permute-start.5) | collective-permute-done | bytes 65568 | tf_op jit(solution)/shard_map/ppermute | solution.py:16
  53.3 1.3 collective-permute-start.6
  54.6 4.2 %collective-permute-start.7 = (f32[1,4,34,1,128]{4,3,2,1,0:T(1,128)S(1)}, f32[1,4,34,1,128]{4,3,2,1,0:T(1,128)S(1)}, u32[]{:S(2)}, u32[]{:S(2)}) collective-permute-start(f32[1,4,34,1,128]{4,3,2,1,0:T(1,128)S(1)} %get-tuple-element.29), channel_id=1, source_target_pairs={{0,1},{2,3},{4,5},{6,7},{8,9},{10,11},{12,13},{14,15},{16,17},{18,... | collective-permute-start | bytes 208904 | tf_op jit(solution)/shard_map/ppermute | solution.py:16
  58.8 1.2 collective-permute-done.7
  59.9 3.6 %select_maximum_fusion.8 = f32[1,4,34,34,130]{4,3,2,1,0:T(8,128)S(1)} fusion(f32[1,4,34,1,128]{4,3,2,1,0:T(1,128)S(1)} %collective-permute-done.6, f32[1,4,34,1,128]{4,3,2,1,0:T(1,128)S(1)} %collective-permute-done.7, f32[1,4,1,32,128]{4,3,2,1,0:T(8,128)S(1)} %collective-permute-done.4, f32[1,4,32,32,128]{4,3,2,1,0:T(8,128)S(1)} %bitcast.25, ...), kind=kLoop, calls=%fused_computation.10 | loop fusion | flops 7213440 | bytes 4771968 | tf_op jit(solution)/shard_map/concatenate | solution.py:20
  63.5 3.0 %pad_maximum_fusion = (f32[1,4,34,33,128]{4,3,2,1,0:T(8,128)}, f32[1,4,34,33,128]{4,3,2,1,0:T(8,128)}) fusion(f32[1,4,34,1,128]{4,3,2,1,0:T(1,128)S(1)} %collective-permute-done.6, f32[1,4,1,32,128]{4,3,2,1,0:T(8,128)S(1)} %collective-permute-done.4, f32[1,4,32,32,128]{4,3,2,1,0:T(8,128)S(1)} %bitcast.26, ...), kind=kLoop, calls=%fused_computation.25 | loop fusion | flops 3446784 | bytes 6963200 | tf_op jit(solution)/shard_map/concatenate | solution.py:20
  66.4 11.2 %add_subtract_fusion.2 = (f32[1,4,32,32,128]{4,3,2,1,0:T(8,128)}, f32[1,4,32,32,128]{4,3,2,1,0:T(8,128)}) fusion(f32[1,4,32,32,128]{4,3,2,1,0:T(8,128)S(1)} %bitcast.27, f32[1,4,1,32,128]{4,3,2,1,0:T(8,128)S(1)} %collective-permute-done.5, f32[1,4,1,32,128]{4,3,2,1,0:T(8,128)S(1)} %collective-permute-done.4, f32[1,4,34,33,128]{4,3,2,1,0:T(8,128)} %get-tuple-element.27, ...), kind=kLoop, calls=%fused_computation.139 | loop fusion | flops 17301504 | bytes 43122688 | tf_op jit(solution)/shard_map/sub | solution.py:74
  77.7 3.0 %add_bitcast_fusion.5 = (f32[1,2,1,32,32,128]{5,4,3,1,2,0:T(8,128)S(1)}, f32[1,2,1,32,32,128]{5,4,3,1,2,0:T(8,128)S(1)}) fusion(f32[1,4,32,32,128]{4,3,2,1,0:T(8,128)} %get-tuple-element.7, f32[1,4,32,32,128]{4,3,2,1,0:T(8,128)} %get-tuple-element.6, f32[1,4,32,32,128]{4,3,2,1,0:T(8,128)S(1)} %bitcast.28, f32[1,4,32,32,128]{4,3,2,1,0:T(8,128)S(1)} %copy-done.2, ...), kind=kLoop, calls=%fused_computation.146 | loop fusion | flops 3407872 | bytes 9961472 | tf_op jit(solution)/shard_map/stack | solution.py:81
  81.0 1.9 collective-permute-start.8
  82.9 3.4 %collective-permute-start.9 = (f32[1,4,1,32,128]{4,3,2,1,0:T(8,128)S(1)}, f32[1,4,1,32,128]{4,3,2,1,0:T(8,128)S(1)}, u32[]{:S(2)}, u32[]{:S(2)}) collective-permute-start(f32[1,4,1,32,128]{4,3,2,1,0:T(8,128)S(1)} %get-tuple-element.35), channel_id=1, source_target_pairs={{0,2},{2,4},{4,6},{6,8},{8,10},{10,12},{12,14},{14,16},{16,18},{18... | collective-permute-start | bytes 196616 | tf_op jit(solution)/shard_map/ppermute | solution.py:16
  86.3 3.7 %collective-permute-done.9 = f32[1,4,1,32,128]{4,3,2,1,0:T(8,128)S(1)} collective-permute-done((f32[1,4,1,32,128]{4,3,2,1,0:T(8,128)S(1)}, f32[1,4,1,32,128]{4,3,2,1,0:T(8,128)S(1)}, u32[]{:S(2)}, u32[]{:S(2)}) %collective-permute-start.9) | collective-permute-done | bytes 65568 | tf_op jit(solution)/shard_map/ppermute | solution.py:16
  90.2 1.3 collective-permute-start.10
  91.5 4.0 %collective-permute-start.11 = (f32[1,4,34,1,128]{4,3,2,1,0:T(1,128)S(1)}, f32[1,4,34,1,128]{4,3,2,1,0:T(1,128)S(1)}, u32[]{:S(2)}, u32[]{:S(2)}) collective-permute-start(f32[1,4,34,1,128]{4,3,2,1,0:T(1,128)S(1)} %get-tuple-element.25), channel_id=1, source_target_pairs={{0,1},{2,3},{4,5},{6,7},{8,9},{10,11},{12,13},{14,15},{16,17},{18,... | collective-permute-start | bytes 208904 | tf_op jit(solution)/shard_map/ppermute | solution.py:16
  95.5 1.3 collective-permute-done.11
  96.8 3.6 %select_maximum_fusion.4 = f32[1,4,34,34,130]{4,3,2,1,0:T(8,128)S(1)} fusion(f32[1,4,34,1,128]{4,3,2,1,0:T(1,128)S(1)} %collective-permute-done.10, f32[1,4,34,1,128]{4,3,2,1,0:T(1,128)S(1)} %collective-permute-done.11, f32[1,4,1,32,128]{4,3,2,1,0:T(8,128)S(1)} %collective-permute-done.8, f32[1,4,32,32,128]{4,3,2,1,0:T(8,128)S(1)} %bitcast.33, ...), kind=kLoop, calls=%fused_computation.6 | loop fusion | flops 7213440 | bytes 4771968 | tf_op jit(solution)/shard_map/concatenate | solution.py:20
  100.4 3.0 %pad_maximum_fusion.1 = (f32[1,4,34,33,128]{4,3,2,1,0:T(8,128)}, f32[1,4,34,33,128]{4,3,2,1,0:T(8,128)}) fusion(f32[1,4,34,1,128]{4,3,2,1,0:T(1,128)S(1)} %collective-permute-done.10, f32[1,4,1,32,128]{4,3,2,1,0:T(8,128)S(1)} %collective-permute-done.8, f32[1,4,32,32,128]{4,3,2,1,0:T(8,128)S(1)} %bitcast.34, ...), kind=kLoop, calls=%fused_computation.27 | loop fusion | flops 3446784 | bytes 6963200 | tf_op jit(solution)/shard_map/concatenate | solution.py:20
  103.4 11.2 %add_subtract_fusion.1 = (f32[1,4,32,32,128]{4,3,2,1,0:T(8,128)}, f32[1,4,32,32,128]{4,3,2,1,0:T(8,128)}) fusion(f32[1,4,32,32,128]{4,3,2,1,0:T(8,128)S(1)} %bitcast.35, f32[1,4,1,32,128]{4,3,2,1,0:T(8,128)S(1)} %collective-permute-done.9, f32[1,4,1,32,128]{4,3,2,1,0:T(8,128)S(1)} %collective-permute-done.8, f32[1,4,34,33,128]{4,3,2,1,0:T(8,128)} %get-tuple-element.23, ...), kind=kLoop, calls=%fused_computation.138 | loop fusion | flops 17301504 | bytes 43122688 | tf_op jit(solution)/shard_map/sub | solution.py:74
  114.6 3.0 %add_bitcast_fusion.3 = (f32[1,2,1,32,32,128]{5,4,3,1,2,0:T(8,128)S(1)}, f32[1,2,1,32,32,128]{5,4,3,1,2,0:T(8,128)S(1)}) fusion(f32[1,4,32,32,128]{4,3,2,1,0:T(8,128)} %get-tuple-element.5, f32[1,4,32,32,128]{4,3,2,1,0:T(8,128)} %get-tuple-element.4, f32[1,4,32,32,128]{4,3,2,1,0:T(8,128)S(1)} %bitcast.36, f32[1,4,32,32,128]{4,3,2,1,0:T(8,128)S(1)} %bitcast.29, ...), kind=kLoop, calls=%fused_computation.144 | loop fusion | flops 3407872 | bytes 9961472 | tf_op jit(solution)/shard_map/stack | solution.py:81
  118.0 1.9 collective-permute-start.12
  119.9 3.6 %collective-permute-start.13 = (f32[1,4,1,32,128]{4,3,2,1,0:T(8,128)S(1)}, f32[1,4,1,32,128]{4,3,2,1,0:T(8,128)S(1)}, u32[]{:S(2)}, u32[]{:S(2)}) collective-permute-start(f32[1,4,1,32,128]{4,3,2,1,0:T(8,128)S(1)} %get-tuple-element.33), channel_id=1, source_target_pairs={{0,2},{2,4},{4,6},{6,8},{8,10},{10,12},{12,14},{14,16},{16,18},{18... | collective-permute-start | bytes 196616 | tf_op jit(solution)/shard_map/ppermute | solution.py:16
  123.5 3.7 %collective-permute-done.13 = f32[1,4,1,32,128]{4,3,2,1,0:T(8,128)S(1)} collective-permute-done((f32[1,4,1,32,128]{4,3,2,1,0:T(8,128)S(1)}, f32[1,4,1,32,128]{4,3,2,1,0:T(8,128)S(1)}, u32[]{:S(2)}, u32[]{:S(2)}) %collective-permute-start.13) | collective-permute-done | bytes 65568 | tf_op jit(solution)/shard_map/ppermute | solution.py:16
  127.3 1.3 collective-permute-start.14
  128.6 4.0 %collective-permute-start.15 = (f32[1,4,34,1,128]{4,3,2,1,0:T(1,128)S(1)}, f32[1,4,34,1,128]{4,3,2,1,0:T(1,128)S(1)}, u32[]{:S(2)}, u32[]{:S(2)}) collective-permute-start(f32[1,4,34,1,128]{4,3,2,1,0:T(1,128)S(1)} %get-tuple-element.21), channel_id=1, source_target_pairs={{0,1},{2,3},{4,5},{6,7},{8,9},{10,11},{12,13},{14,15},{16,17},{18,... | collective-permute-start | bytes 208904 | tf_op jit(solution)/shard_map/ppermute | solution.py:16
  133.3 0.7 collective-permute-done.15
  134.0 3.6 %select_maximum_fusion = f32[1,4,34,34,130]{4,3,2,1,0:T(8,128)S(1)} fusion(f32[1,4,34,1,128]{4,3,2,1,0:T(1,128)S(1)} %collective-permute-done.14, f32[1,4,34,1,128]{4,3,2,1,0:T(1,128)S(1)} %collective-permute-done.15, f32[1,4,1,32,128]{4,3,2,1,0:T(8,128)S(1)} %collective-permute-done.12, f32[1,4,32,32,128]{4,3,2,1,0:T(8,128)S(1)} %bitcast.41, ...), kind=kLoop, calls=%fused_computation.2 | loop fusion | flops 7213440 | bytes 4771968 | tf_op jit(solution)/shard_map/concatenate | solution.py:20
  137.6 3.0 %pad_maximum_fusion.2 = (f32[1,4,34,33,128]{4,3,2,1,0:T(8,128)}, f32[1,4,34,33,128]{4,3,2,1,0:T(8,128)}) fusion(f32[1,4,34,1,128]{4,3,2,1,0:T(1,128)S(1)} %collective-permute-done.14, f32[1,4,1,32,128]{4,3,2,1,0:T(8,128)S(1)} %collective-permute-done.12, f32[1,4,32,32,128]{4,3,2,1,0:T(8,128)S(1)} %bitcast.42, ...), kind=kLoop, calls=%fused_computation.29 | loop fusion | flops 3446784 | bytes 6963200 | tf_op jit(solution)/shard_map/concatenate | solution.py:20
  140.6 13.1 %add_subtract_fusion = (f32[1,4,32,32,128]{4,3,2,1,0:T(8,128)}, f32[1,4,32,32,128]{4,3,2,1,0:T(8,128)}) fusion(f32[1,4,32,32,128]{4,3,2,1,0:T(8,128)} %bitcast.43, f32[1,4,1,32,128]{4,3,2,1,0:T(8,128)S(1)} %collective-permute-done.13, f32[1,4,1,32,128]{4,3,2,1,0:T(8,128)S(1)} %collective-permute-done.12, f32[1,4,34,33,128]{4,3,2,1,0:T(8,128)} %get-tuple-element.19, ...), kind=kLoop, calls=%fused_computation.137 | loop fusion | flops 17301504 | bytes 43122688 | tf_op jit(solution)/shard_map/sub | solution.py:74
  153.6 3.6 %add_bitcast_fusion.1 = (f32[1,2,1,32,32,128]{5,4,3,1,2,0:T(8,128)S(1)}, f32[1,2,1,32,32,128]{5,4,3,1,2,0:T(8,128)S(1)}) fusion(f32[1,4,32,32,128]{4,3,2,1,0:T(8,128)} %bitcast.44, f32[1,4,32,32,128]{4,3,2,1,0:T(8,128)} %get-tuple-element.3, f32[1,4,32,32,128]{4,3,2,1,0:T(8,128)} %get-tuple-element.2, f32[1,4,32,32,128]{4,3,2,1,0:T(8,128)S(1)} %bitcast.37, ...), kind=kLoop, calls=%fused_computation.142 | loop fusion | flops 3407872 | bytes 9961472 | tf_op jit(solution)/shard_map/stack | solution.py:81
  157.6 1.3 copy-done.12
  158.9 0.8 copy-done.1
  159.8 1.3 fusion.55
  161.1 51.8 %all-reduce.6.cloned.1.call-done = f32[32,32,128]{2,1,0:T(8,128)} async-done(((f32[32,32,128]{2,1,0:T(8,128)}), f32[32,32,128]{2,1,0:T(8,128)}) %all-reduce.6.cloned.1.call-update) | async-done | bytes 524304 | tf_op jit(solution)/shard_map/psum | solution.py:98
  212.8 1.9 broadcast_multiply_fusion
  (55 shorter events, 1.8 us)
Async XLA Ops:
  7.2 205.7 %all-reduce.6.cloned.1.call-start = ((), (), s32[]{:S(2)}) async-start(), calls=%async_computation | async-start | bytes 1048576 | tf_op jit(solution)/shard_map/psum | solution.py:98
  8.1 13.7 %collective-permute-start.1 = (f32[1,4,1,32,128]{4,3,2,1,0:T(8,128)S(1)}, f32[1,4,1,32,128]{4,3,2,1,0:T(8,128)S(1)}, u32[]{:S(2)}, u32[]{:S(2)}) collective-permute-start(f32[1,4,1,32,128]{4,3,2,1,0:T(8,128)S(1)} %get-tuple-element.39), channel_id=1, source_target_pairs={{0,2},{2,4},{4,6},{6,8},{8,10},{10,12},{12,14},{14,16},{16,18},{18... | collective-permute-start | bytes 196616 | tf_op jit(solution)/shard_map/ppermute | solution.py:16
  11.3 10.5 %copy-start.2 = (f32[1,4,32,32,128]{4,3,2,1,0:T(8,128)S(1)}, f32[1,4,32,32,128]{4,3,2,1,0:T(8,128)}, u32[]{:S(2)}) copy-start(f32[1,4,32,32,128]{4,3,2,1,0:T(8,128)} %param.8) | copy-start | bytes 6291460
  11.3 10.7 %collective-permute-start = (f32[1,4,1,32,128]{4,3,2,1,0:T(8,128)S(1)}, f32[1,4,1,32,128]{4,3,2,1,0:T(8,128)S(1)}, u32[]{:S(2)}, u32[]{:S(2)}) collective-permute-start(f32[1,4,1,32,128]{4,3,2,1,0:T(8,128)S(1)} %get-tuple-element.38), channel_id=1, source_target_pairs={{2,0},{4,2},{6,4},{8,6},{10,8},{12,10},{14,12},{16,14},{18,16},{20... | collective-permute-start | bytes 196616 | tf_op jit(solution)/shard_map/ppermute | solution.py:19
  21.7 10.0 %copy-start.3 = (f32[32,32,128]{2,1,0:T(8,128)}, f32[32,32,128]{2,1,0:T(8,128)S(1)}, u32[]{:S(2)}) copy-start(f32[32,32,128]{2,1,0:T(8,128)S(1)} %get-tuple-element.40) | copy-start | bytes 1572868
  21.7 10.0 %copy-start.4 = (f32[32,32,128]{2,1,0:T(8,128)}, f32[32,32,128]{2,1,0:T(8,128)S(1)}, u32[]{:S(2)}) copy-start(f32[32,32,128]{2,1,0:T(8,128)S(1)} %get-tuple-element.41) | copy-start | bytes 1572868
  21.7 10.0 %copy-start.5 = (f32[32,32,128]{2,1,0:T(8,128)}, f32[32,32,128]{2,1,0:T(8,128)S(1)}, u32[]{:S(2)}) copy-start(f32[32,32,128]{2,1,0:T(8,128)S(1)} %get-tuple-element.42) | copy-start | bytes 1572868
  21.8 10.0 %copy-start.6 = (f32[32,32,128]{2,1,0:T(8,128)}, f32[32,32,128]{2,1,0:T(8,128)S(1)}, u32[]{:S(2)}) copy-start(f32[32,32,128]{2,1,0:T(8,128)S(1)} %get-tuple-element.43) | copy-start | bytes 1572868
  21.8 10.0 %copy-start.7 = (f32[32,32,128]{2,1,0:T(8,128)}, f32[32,32,128]{2,1,0:T(8,128)S(1)}, u32[]{:S(2)}) copy-start(f32[32,32,128]{2,1,0:T(8,128)S(1)} %get-tuple-element.44) | copy-start | bytes 1572868
  21.8 10.0 %copy-start.8 = (f32[32,32,128]{2,1,0:T(8,128)}, f32[32,32,128]{2,1,0:T(8,128)S(1)}, u32[]{:S(2)}) copy-start(f32[32,32,128]{2,1,0:T(8,128)S(1)} %get-tuple-element.45) | copy-start | bytes 1572868
  21.8 5.8 %copy-start.13 = (f32[32,32,128]{2,1,0:T(8,128)S(1)}, f32[32,32,128]{2,1,0:T(8,128)}, u32[]{:S(2)}) copy-start(f32[32,32,128]{2,1,0:T(8,128)} %param.12) | copy-start | bytes 1572868
  21.8 5.8 %copy-start.14 = (f32[32,32,128]{2,1,0:T(8,128)S(1)}, f32[32,32,128]{2,1,0:T(8,128)}, u32[]{:S(2)}) copy-start(f32[32,32,128]{2,1,0:T(8,128)} %param.11) | copy-start | bytes 1572868
  22.2 5.7 %collective-permute-start.2 = (f32[1,4,34,1,128]{4,3,2,1,0:T(1,128)S(1)}, f32[1,4,34,1,128]{4,3,2,1,0:T(1,128)S(1)}, u32[]{:S(2)}, u32[]{:S(2)}) collective-permute-start(f32[1,4,34,1,128]{4,3,2,1,0:T(1,128)S(1)} %get-tuple-element.31), channel_id=1, source_target_pairs={{1,0},{3,2},{5,4},{7,6},{9,8},{11,10},{13,12},{15,14},{17,16},{19,... | collective-permute-start | bytes 208904 | tf_op jit(solution)/shard_map/ppermute | solution.py:19
  23.6 5.3 %collective-permute-start.3 = (f32[1,4,34,1,128]{4,3,2,1,0:T(1,128)S(1)}, f32[1,4,34,1,128]{4,3,2,1,0:T(1,128)S(1)}, u32[]{:S(2)}, u32[]{:S(2)}) collective-permute-start(f32[1,4,34,1,128]{4,3,2,1,0:T(1,128)S(1)} %get-tuple-element.30), channel_id=1, source_target_pairs={{0,1},{2,3},{4,5},{6,7},{8,9},{10,11},{12,13},{14,15},{16,17},{18,... | collective-permute-start | bytes 208904 | tf_op jit(solution)/shard_map/ppermute | solution.py:16
  27.9 12.4 %copy-start.9 = (f32[32,32,128]{2,1,0:T(8,128)}, f32[32,32,128]{2,1,0:T(8,128)S(1)}, u32[]{:S(2)}) copy-start(f32[32,32,128]{2,1,0:T(8,128)S(1)} %get-tuple-element.46) | copy-start | bytes 1572868
  27.9 12.4 %copy-start.10 = (f32[32,32,128]{2,1,0:T(8,128)}, f32[32,32,128]{2,1,0:T(8,128)S(1)}, u32[]{:S(2)}) copy-start(f32[32,32,128]{2,1,0:T(8,128)S(1)} %get-tuple-element.47) | copy-start | bytes 1572868
  31.8 8.5 %copy-start.11 = (f32[32,32,128]{2,1,0:T(8,128)S(1)}, f32[32,32,128]{2,1,0:T(8,128)}, u32[]{:S(2)}) copy-start(f32[32,32,128]{2,1,0:T(8,128)} %param.10) | copy-start | bytes 1572868
  43.2 5.3 %collective-permute-start.4 = (f32[1,4,1,32,128]{4,3,2,1,0:T(8,128)S(1)}, f32[1,4,1,32,128]{4,3,2,1,0:T(8,128)S(1)}, u32[]{:S(2)}, u32[]{:S(2)}) collective-permute-start(f32[1,4,1,32,128]{4,3,2,1,0:T(8,128)S(1)} %get-tuple-element.36), channel_id=1, source_target_pairs={{2,0},{4,2},{6,4},{8,6},{10,8},{12,10},{14,12},{16,14},{18,16},{20... | collective-permute-start | bytes 196616 | tf_op jit(solution)/shard_map/ppermute | solution.py:19
  46.0 7.1 %collective-permute-start.5 = (f32[1,4,1,32,128]{4,3,2,1,0:T(8,128)S(1)}, f32[1,4,1,32,128]{4,3,2,1,0:T(8,128)S(1)}, u32[]{:S(2)}, u32[]{:S(2)}) collective-permute-start(f32[1,4,1,32,128]{4,3,2,1,0:T(8,128)S(1)} %get-tuple-element.37), channel_id=1, source_target_pairs={{0,2},{2,4},{4,6},{6,8},{8,10},{10,12},{12,14},{14,16},{16,18},{18... | collective-permute-start | bytes 196616 | tf_op jit(solution)/shard_map/ppermute | solution.py:16
  53.3 5.5 %collective-permute-start.6 = (f32[1,4,34,1,128]{4,3,2,1,0:T(1,128)S(1)}, f32[1,4,34,1,128]{4,3,2,1,0:T(1,128)S(1)}, u32[]{:S(2)}, u32[]{:S(2)}) collective-permute-start(f32[1,4,34,1,128]{4,3,2,1,0:T(1,128)S(1)} %get-tuple-element.28), channel_id=1, source_target_pairs={{1,0},{3,2},{5,4},{7,6},{9,8},{11,10},{13,12},{15,14},{17,16},{19,... | collective-permute-start | bytes 208904 | tf_op jit(solution)/shard_map/ppermute | solution.py:19
  54.6 5.3 %collective-permute-start.7 = (f32[1,4,34,1,128]{4,3,2,1,0:T(1,128)S(1)}, f32[1,4,34,1,128]{4,3,2,1,0:T(1,128)S(1)}, u32[]{:S(2)}, u32[]{:S(2)}) collective-permute-start(f32[1,4,34,1,128]{4,3,2,1,0:T(1,128)S(1)} %get-tuple-element.29), channel_id=1, source_target_pairs={{0,1},{2,3},{4,5},{6,7},{8,9},{10,11},{12,13},{14,15},{16,17},{18,... | collective-permute-start | bytes 208904 | tf_op jit(solution)/shard_map/ppermute | solution.py:16
  81.0 5.3 %collective-permute-start.8 = (f32[1,4,1,32,128]{4,3,2,1,0:T(8,128)S(1)}, f32[1,4,1,32,128]{4,3,2,1,0:T(8,128)S(1)}, u32[]{:S(2)}, u32[]{:S(2)}) collective-permute-start(f32[1,4,1,32,128]{4,3,2,1,0:T(8,128)S(1)} %get-tuple-element.34), channel_id=1, source_target_pairs={{2,0},{4,2},{6,4},{8,6},{10,8},{12,10},{14,12},{16,14},{18,16},{20... | collective-permute-start | bytes 196616 | tf_op jit(solution)/shard_map/ppermute | solution.py:19
  82.9 7.1 %collective-permute-start.9 = (f32[1,4,1,32,128]{4,3,2,1,0:T(8,128)S(1)}, f32[1,4,1,32,128]{4,3,2,1,0:T(8,128)S(1)}, u32[]{:S(2)}, u32[]{:S(2)}) collective-permute-start(f32[1,4,1,32,128]{4,3,2,1,0:T(8,128)S(1)} %get-tuple-element.35), channel_id=1, source_target_pairs={{0,2},{2,4},{4,6},{6,8},{8,10},{10,12},{12,14},{14,16},{16,18},{18... | collective-permute-start | bytes 196616 | tf_op jit(solution)/shard_map/ppermute | solution.py:16
  90.2 5.3 %collective-permute-start.10 = (f32[1,4,34,1,128]{4,3,2,1,0:T(1,128)S(1)}, f32[1,4,34,1,128]{4,3,2,1,0:T(1,128)S(1)}, u32[]{:S(2)}, u32[]{:S(2)}) collective-permute-start(f32[1,4,34,1,128]{4,3,2,1,0:T(1,128)S(1)} %get-tuple-element.24), channel_id=1, source_target_pairs={{1,0},{3,2},{5,4},{7,6},{9,8},{11,10},{13,12},{15,14},{17,16},{19,... | collective-permute-start | bytes 208904 | tf_op jit(solution)/shard_map/ppermute | solution.py:19
  91.5 5.3 %collective-permute-start.11 = (f32[1,4,34,1,128]{4,3,2,1,0:T(1,128)S(1)}, f32[1,4,34,1,128]{4,3,2,1,0:T(1,128)S(1)}, u32[]{:S(2)}, u32[]{:S(2)}) collective-permute-start(f32[1,4,34,1,128]{4,3,2,1,0:T(1,128)S(1)} %get-tuple-element.25), channel_id=1, source_target_pairs={{0,1},{2,3},{4,5},{6,7},{8,9},{10,11},{12,13},{14,15},{16,17},{18,... | collective-permute-start | bytes 208904 | tf_op jit(solution)/shard_map/ppermute | solution.py:16
  117.9 19.6 %copy-start = (f32[1,2,2,32,32,128]{5,4,3,2,1,0:T(8,128)}, f32[1,2,2,32,32,128]{5,4,3,2,1,0:T(8,128)S(1)}, u32[]{:S(2)}) copy-start(f32[1,2,2,32,32,128]{5,4,3,2,1,0:T(8,128)S(1)} %copy.14) | copy-start | bytes 6291460
  118.0 5.5 %collective-permute-start.12 = (f32[1,4,1,32,128]{4,3,2,1,0:T(8,128)S(1)}, f32[1,4,1,32,128]{4,3,2,1,0:T(8,128)S(1)}, u32[]{:S(2)}, u32[]{:S(2)}) collective-permute-start(f32[1,4,1,32,128]{4,3,2,1,0:T(8,128)S(1)} %get-tuple-element.32), channel_id=1, source_target_pairs={{2,0},{4,2},{6,4},{8,6},{10,8},{12,10},{14,12},{16,14},{18,16},{20... | collective-permute-start | bytes 196616 | tf_op jit(solution)/shard_map/ppermute | solution.py:19
  119.9 7.3 %collective-permute-start.13 = (f32[1,4,1,32,128]{4,3,2,1,0:T(8,128)S(1)}, f32[1,4,1,32,128]{4,3,2,1,0:T(8,128)S(1)}, u32[]{:S(2)}, u32[]{:S(2)}) collective-permute-start(f32[1,4,1,32,128]{4,3,2,1,0:T(8,128)S(1)} %get-tuple-element.33), channel_id=1, source_target_pairs={{0,2},{2,4},{4,6},{6,8},{8,10},{10,12},{12,14},{14,16},{16,18},{18... | collective-permute-start | bytes 196616 | tf_op jit(solution)/shard_map/ppermute | solution.py:16
  127.3 5.9 %collective-permute-start.14 = (f32[1,4,34,1,128]{4,3,2,1,0:T(1,128)S(1)}, f32[1,4,34,1,128]{4,3,2,1,0:T(1,128)S(1)}, u32[]{:S(2)}, u32[]{:S(2)}) collective-permute-start(f32[1,4,34,1,128]{4,3,2,1,0:T(1,128)S(1)} %get-tuple-element.20), channel_id=1, source_target_pairs={{1,0},{3,2},{5,4},{7,6},{9,8},{11,10},{13,12},{15,14},{17,16},{19,... | collective-permute-start | bytes 208904 | tf_op jit(solution)/shard_map/ppermute | solution.py:19
  128.6 5.3 %collective-permute-start.15 = (f32[1,4,34,1,128]{4,3,2,1,0:T(1,128)S(1)}, f32[1,4,34,1,128]{4,3,2,1,0:T(1,128)S(1)}, u32[]{:S(2)}, u32[]{:S(2)}) collective-permute-start(f32[1,4,34,1,128]{4,3,2,1,0:T(1,128)S(1)} %get-tuple-element.21), channel_id=1, source_target_pairs={{0,1},{2,3},{4,5},{6,7},{8,9},{10,11},{12,13},{14,15},{16,17},{18,... | collective-permute-start | bytes 208904 | tf_op jit(solution)/shard_map/ppermute | solution.py:16
  157.4 2.3 %copy-start.1 = (f32[1,2,2,32,32,128]{5,4,3,2,1,0:T(8,128)S(1)}, f32[1,2,2,32,32,128]{5,4,3,2,1,0:T(8,128)}, u32[]{:S(2)}) copy-start(f32[1,2,2,32,32,128]{5,4,3,2,1,0:T(8,128)} %copy-done) | copy-start | bytes 6291460
  157.6 1.3 copy-start.12
Sparse Core Ops, SparseCore 0:
  161.2 51.5 all-reduce.5
where the time goes:
time: 223 us; the launch traced here: 222 us
  other arithmetic  88.9 us (40%)
  waiting for transfers between devices  68.2 us (31%)
  starting transfers between devices  45.1 us (20%)
  between operations  15.3 us (7%)
  local copies, waits for them, and re-layouts  4.16 us (2%)
    psum x1, waiting for transfers between devices, local(): image = lax.psum(covered * correlation, 'shot') / ITERS  51.8 us
    sub x4, other arithmetic, advance(): across = second_x + second_y + second_z - along  44 us
    ppermute x8, starting transfers between devices, extended(): lax.ppermute(lax.slice_in_dim(block, block.shape[dim] - width, None, axis...  28.8 us
    concatenate x7, other arithmetic, extended(): block = jnp.concatenate([low, block, high], axis=dim)  22.4 us
    ppermute x8, waiting for transfers between devices, extended(): lax.ppermute(lax.slice_in_dim(block, block.shape[dim] - width, None, axis...  16.3 us
    ppermute x8, starting transfers between devices, extended(): lax.ppermute(lax.slice_in_dim(block, 0, width, axis=dim), axis, backward)  16.3 us
    another operation x8, other arithmetic, advance(): return jnp.stack([next_p, next_q], axis=2).reshape(centre.shape)  12.8 us
    mul x1, other arithmetic, advance(): normal_x * normal_x * second_x + normal_y * normal_y * second_y  6.06 us
  transfers between devices with their start and end apart: 17, of which 9 were waited for; matrix products, arithmetic and copies ran while one was open for 3% of the time, Pallas kernels for 0%

commit v1 on v0

v1 whole, which is shorter than its diff:
```python
import functools
import math

import jax
import jax.numpy as jnp
from jax import lax
from jax.experimental import pallas as pl
from jax.experimental.pallas import tpu as pltpu
from jax.sharding import PartitionSpec as P

ITERS = 4
F = 4
PAD = 8
MESH = pl.DeviceIdType.MESH
NK = 12
AXX, AYY, BXY, AP, AM, BP, BM, CP, CM, CG, CR, CV = range(NK)


def sin_poly(x, x2):
    return x * (1.0 + x2 * (-1.0 / 6 + x2 * (1.0 / 120 + x2 * (-1.0 / 5040 + x2 * (1.0 / 362880 - x2 * (1.0 / 39916800))))))


def cos_poly(x2):
    return 1.0 + x2 * (-0.5 + x2 * (1.0 / 24 + x2 * (-1.0 / 720 + x2 * (1.0 / 40320 + x2 * (-1.0 / 3628800 + x2 * (1.0 / 479001600))))))


def normals(tilt, azimuth):
    theta = tilt.astype(jnp.float32) * (math.pi / 180.0)
    t2 = theta * theta
    sin_t, cos_t = sin_poly(theta, t2), cos_poly(t2)
    b1, b2, b3, b4 = (azimuth >= edge for edge in (45, 135, 225, 315))
    zero, step = jnp.zeros_like(azimuth), jnp.full_like(azimuth, 90)
    base = jnp.where(b1, step, zero) + jnp.where(b2, step, zero) + jnp.where(b3, step, zero) + jnp.where(b4, step, zero)
    rest = (azimuth - base).astype(jnp.float32) * (math.pi / 180.0)
    r2 = rest * rest
    s, c = sin_poly(rest, r2), cos_poly(r2)
    odd = (base == 90) | (base == 270)
    sin_m = jnp.where(odd, c, s)
    cos_m = jnp.where(odd, s, c)
    sin_neg = (base == 180) | (base == 270)
    cos_neg = (base == 90) | (base == 180)
    sin_p = jnp.where(sin_neg, -sin_m, sin_m)
    cos_p = jnp.where(cos_neg, -cos_m, cos_m)
    return sin_t * cos_p, sin_t * sin_p, cos_t


def kernel(sizes, now, prev, vel, eps, dlt, tilt, azim, aper, wave_out, img_out,
           U, M, A, K, corr, P_, Q, PC, QC, R1, R2, IMG, local, ssem, rsem, isem, osem):
    ngx, X, Y, Z = sizes
    T = Y // 8
    shot, gx, gy = lax.axis_index("shot"), lax.axis_index("gx"), lax.axis_index("gy")
    has_l, has_r = gx > 0, gx < ngx - 1
    core = lax.rem(shot, 2)
    core_pair = shot + 1 - 2 * core
    z_pair = lax.rem(shot + 2, 4)
    left, right, other = gx - 1, gx + 1, 1 - gy
    dev_l, dev_r, dev_y = (shot, left, gy), (shot, right, gy), (shot, gx, other)
    dev_dl, dev_dr = (shot, left, other), (shot, right, other)
    dev_c, dev_z = (core_pair, gx, gy), (z_pair, gx, gy)
    y_send = PAD + (Y - 1) * (1 - gy)
    y_recv = PAD - 1 + (Y + 1) * (1 - gy)

    loads = [pltpu.make_async_copy(now.at[0], U.at[0, :, pl.ds(1, X), pl.ds(PAD, Y), :], local.at[0])]
    for i, ref in enumerate((tilt, azim)):
        loads.append(pltpu.make_async_copy(ref, A.at[i], local.at[1 + i]))
    for i, ref in enumerate((vel, eps, dlt)):
        loads.append(pltpu.make_async_copy(ref, M.at[i], local.at[3 + i]))
    loads.append(pltpu.make_async_copy(prev.at[0], U.at[1, :, pl.ds(1, X), pl.ds(PAD, Y), :], local.at[6]))
    for copy in loads:
        copy.start()

    barrier = pltpu.get_barrier_semaphore()

    def hello(dev):
        pl.semaphore_signal(barrier, inc=1, device_id=dev, device_id_type=MESH)

    for dev in (dev_y, dev_c, dev_z):
        hello(dev)

    @pl.when(has_l)
    def _():
        hello(dev_l)
        hello(dev_dl)

    @pl.when(has_r)
    def _():
        hello(dev_r)
        hello(dev_dr)

    zero_tile = jnp.zeros((8, Z), jnp.float32)

    def zero_rows(x, c):
        for par in range(2):
            for f in range(F):
                U[par, f, x, pl.ds(0, 8), :] = zero_tile
                U[par, f, x, pl.ds(PAD + Y, 8), :] = zero_tile
        return c

    lax.fori_loop(0, X + 2, zero_rows, 0)

    def zero_plane(x):
        for par in range(2):
            for f in range(F):
                for j in range(T):
                    U[par, f, x, pl.ds(PAD + 8 * j, 8), :] = zero_tile

    @pl.when(jnp.logical_not(has_l))
    def _():
        zero_plane(0)

    @pl.when(jnp.logical_not(has_r))
    def _():
        zero_plane(X + 1)

    pl.semaphore_wait(barrier, 3 + 2 * has_l.astype(jnp.int32) + 2 * has_r.astype(jnp.int32))

    def halo(t, d):
        par = t % 2

        def plane(x):
            if t == 0:
                return now.at[0, :, x - 1]
            return U.at[par, :, x, pl.ds(PAD, Y), :]

        def make(d, src, dst, dev):
            return pltpu.make_async_remote_copy(
                src_ref=src, dst_ref=dst, send_sem=ssem.at[t, d], recv_sem=rsem.at[t, d],
                device_id=dev, device_id_type=MESH)

        if d == 0:
            return make(0, plane(1), U.at[par, :, X + 1, pl.ds(PAD, Y), :], dev_l)
        if d == 1:
            return make(1, plane(X), U.at[par, :, 0, pl.ds(PAD, Y), :], dev_r)
        if d == 2:
            return make(2, P_.at[t], Q.at[t], dev_y)
        if d == 3:
            return make(3, PC.at[t, 0], QC.at[t, 1], dev_dl)
        return make(4, PC.at[t, 1], QC.at[t, 0], dev_dr)

    def send_x(t):
        @pl.when(has_l)
        def _():
            halo(t, 0).start()

        @pl.when(has_r)
        def _():
            halo(t, 1).start()

    def send_y(t):
        par = t % 2
        for f in range(F):
            P_[t, f] = U[par, f, pl.ds(1, X), y_send, :]
            PC[t, 0, pl.ds(f, 1), :] = U[par, f, 1, pl.ds(y_send, 1), :]
            PC[t, 1, pl.ds(f, 1), :] = U[par, f, X, pl.ds(y_send, 1), :]
        halo(t, 2).start()

        @pl.when(has_l)
        def _():
            halo(t, 3).start()

        @pl.when(has_r)
        def _():
            halo(t, 4).start()

    def receive(t):
        par = t % 2
        halo(t, 2).wait_recv()
        for f in range(F):
            U[par, f, pl.ds(1, X), y_recv, :] = Q[t, f]

        @pl.when(has_r)
        def _():
            halo(t, 0).wait_recv()
            halo(t, 3).wait_recv()
            for f in range(F):
                U[par, f, X + 1, pl.ds(y_recv, 1), :] = QC[t, 1, pl.ds(f, 1), :]

        @pl.when(has_l)
        def _():
            halo(t, 1).wait_recv()
            halo(t, 4).wait_recv()
            for f in range(F):
                U[par, f, 0, pl.ds(y_recv, 1), :] = QC[t, 0, pl.ds(f, 1), :]

    def sent(t):
        halo(t, 2).wait_send()

        @pl.when(has_l)
        def _():
            halo(t, 0).wait_send()
            halo(t, 3).wait_send()

        @pl.when(has_r)
        def _():
            halo(t, 1).wait_send()
            halo(t, 4).wait_send()

    send_x(0)
    loads[0].wait()
    send_y(0)

    lane = lax.broadcasted_iota(jnp.int32, (8, Z), 1)
    mask_p = jnp.where(lane == 0, 0.0, 1.0)
    mask_m = jnp.where(lane == Z - 1, 0.0, 1.0)
    for i in range(1, 6):
        loads[i].wait()

    def model(x, c):
        for j in range(T):
            rows = pl.ds(8 * j, 8)
            n_x, n_y, n_z = normals(A[0, x, rows, :], A[1, x, rows, :])
            v = M[0, x, rows, :]
            gain = 1.0 + 2.0 * M[1, x, rows, :]
            root = jnp.sqrt(1.0 + 2.0 * M[2, x, rows, :])
            half = 0.5 * n_z
            zz, xz, yz = n_z * n_z, half * n_x, half * n_y
            K[AXX, x, rows, :] = n_x * n_x
            K[AYY, x, rows, :] = n_y * n_y
            K[BXY, x, rows, :] = 0.5 * n_x * n_y
            for value, plus, minus in ((zz, AP, AM), (xz, BP, BM), (yz, CP, CM)):
                K[plus, x, rows, :] = pltpu.roll(value, 1, 1) * mask_p
                K[minus, x, rows, :] = pltpu.roll(value, Z - 1, 1) * mask_m
            K[CG, x, rows, :] = v * gain
            K[CR, x, rows, :] = v * root
            K[CV, x, rows, :] = v
        return c

    lax.fori_loop(0, X, model, 0)
    loads[6].wait()
    covered = aper[0, 0, 0].astype(jnp.float32) * (1.0 / ITERS)

    def segment(t, row, first, count, unroll):
        a, b = t % 2, 1 - t % 2
        row = pl.multiple_of(row, 8)
        yrow = pl.multiple_of(row - PAD, 8)

        def plane(f, x):
            mid = U[a, f, x, pl.ds(row, 8), :]
            up, down = U[a, f, x, pl.ds(row + 1, 8), :], U[a, f, x, pl.ds(row - 1, 8), :]
            return mid, up - down, up + down

        def body(x, carry):
            rows = pl.ds(yrow, 8)
            k = [K[i, x - 1, rows, :] for i in range(NK)]
            cxx, cyy = 1.0 - k[AXX], 1.0 - k[AYY]
            cap, cam = mask_p - k[AP], mask_m - k[AM]
            ahead, fresh, op = [], [], []
            for f in range(F):
                f0, e0, f1, e1, ys = carry[f]
                f2, e2, ys2 = plane(f, x + 1)
                ahead.append((f1, e1, f2, e2, ys2))
                xs, dx, exy = f2 + f0, f2 - f0, e2 - e0
                tp = k[BP] * dx + k[CP] * e1
                tm = k[BM] * dx + k[CM] * e1
                mix = k[BXY] * exy
                if f % 2 == 0:
                    sp, sm = cap * f1 - tp, cam * f1 + tm
                    side = cxx * xs + cyy * ys - mix
                else:
                    sp, sm = k[AP] * f1 + tp, k[AM] * f1 - tm
                    side = k[AXX] * xs + k[AYY] * ys + mix
                op.append(side + (pltpu.roll(sp, Z - 1, 1) + pltpu.roll(sm, 1, 1)))
            for pair in range(F // 2):
                p, q = carry[2 * pair][2], carry[2 * pair + 1][2]
                p2, q2 = p + p, q + q
                across = op[2 * pair] - (p2 + p2)
                along = op[2 * pair + 1] - q2
                p_old = U[b, 2 * pair, x, pl.ds(row, 8), :]
                q_old = U[b, 2 * pair + 1, x, pl.ds(row, 8), :]
                p_new = (p2 - p_old) + (k[CG] * across + k[CR] * along)
                q_new = (q2 - q_old) + (k[CR] * across + k[CV] * along)
                U[b, 2 * pair, x, pl.ds(row, 8), :] = p_new
                U[b, 2 * pair + 1, x, pl.ds(row, 8), :] = q_new
                fresh.append(p_new)
            prod = fresh[0] * fresh[1]
            if t > 0:
                prod = prod + corr[x - 1, rows, :]
            if t == ITERS - 1:
                prod = prod * covered
            corr[x - 1, rows, :] = prod
            return tuple(ahead)

        def start(f):
            f0, e0, _ = plane(f, first - 1)
            return (f0, e0) + plane(f, first)

        carry = tuple(start(f) for f in range(F))

        def several(i, carry):
            for u in range(unroll):
                carry = body(first + i * unroll + u, carry)
            return carry

        if count == unroll:
            several(0, carry)
        else:
            lax.fori_loop(0, count // unroll, several, carry)

    edge_row = PAD + (Y - 8) * (1 - gy)
    inner_row = PAD + 8 * gy
    for t in range(ITERS):
        receive(t)
        if t > 0:
            sent(t - 1)
        segment(t, edge_row, 1, X, 2)

        def ends(k, c, t=t):
            segment(t, inner_row + 8 * k, 1, 1, 1)
            segment(t, inner_row + 8 * k, X, 1, 1)
            return c

        lax.fori_loop(0, T - 1, ends, 0)
        if t < ITERS - 1:
            send_x(t + 1)
            send_y(t + 1)

        def inner(k, c, t=t):
            segment(t, inner_row + 8 * k, 2, X - 2, 2)
            return c

        lax.fori_loop(0, T - 1, inner, 0)
    sent(ITERS - 1)

    last = ITERS % 2
    store = pltpu.make_async_copy(U.at[last, :, pl.ds(1, X), pl.ds(PAD, Y), :], wave_out.at[0], osem.at[0])
    store.start()

    H = X // 2
    mine, theirs = pl.ds(core * H, H), pl.ds((1 - core) * H, H)

    def image_copy(i, src, dst, dev):
        return pltpu.make_async_remote_copy(
            src_ref=src, dst_ref=dst, send_sem=isem.at[0, i], recv_sem=isem.at[1, i],
            device_id=dev, device_id_type=MESH)

    first = image_copy(0, corr.at[theirs], R1, dev_c)
    first.start()
    first.wait()

    def add1(x, c):
        for j in range(T):
            rows = pl.ds(8 * j, 8)
            R1[x, rows, :] = R1[x, rows, :] + corr[core * H + x, rows, :]
        return c

    lax.fori_loop(0, H, add1, 0)
    second = image_copy(1, R1, R2, dev_z)
    second.start()
    second.wait()

    def add2(x, c):
        for j in range(T):
            rows = pl.ds(8 * j, 8)
            IMG[core * H + x, rows, :] = R1[x, rows, :] + R2[x, rows, :]
        return c

    lax.fori_loop(0, H, add2, 0)
    third = image_copy(2, IMG.at[mine], IMG.at[mine], dev_c)
    third.start()
    third.wait()
    out = pltpu.make_async_copy(IMG, img_out, osem.at[1])
    out.start()
    out.wait()
    store.wait()


def solution(mesh):
    ngx = mesh.shape["gx"]

    def local(now, prev, vel, eps, dlt, tilt, azim, aper):
        X, Y, Z = vel.shape
        any_, vm = pl.BlockSpec(memory_space=pl.ANY), pltpu.VMEM
        f32 = jnp.float32
        return pl.pallas_call(
            functools.partial(kernel, (ngx, X, Y, Z)),
            out_shape=(jax.ShapeDtypeStruct(now.shape, f32), jax.ShapeDtypeStruct(vel.shape, f32)),
            in_specs=[any_] * 7 + [pl.BlockSpec(memory_space=pltpu.SMEM)],
            out_specs=(any_, any_),
            scratch_shapes=[
                vm((2, F, X + 2, Y + 2 * PAD, Z), f32),
                vm((3, X, Y, Z), f32),
                vm((2, X, Y, Z), jnp.int32),
                vm((NK, X, Y, Z), f32),
                vm((X, Y, Z), f32),
                vm((ITERS, F, X, Z), f32),
                vm((ITERS, F, X, Z), f32),
                vm((ITERS, 2, F, Z), f32),
                vm((ITERS, 2, F, Z), f32),
                vm((X // 2, Y, Z), f32),
                vm((X // 2, Y, Z), f32),
                vm((X, Y, Z), f32),
                pltpu.SemaphoreType.DMA((7,)),
                pltpu.SemaphoreType.DMA((ITERS, 5)),
                pltpu.SemaphoreType.DMA((ITERS, 5)),
                pltpu.SemaphoreType.DMA((2, 3)),
                pltpu.SemaphoreType.DMA((2,)),
            ],
            compiler_params=pltpu.CompilerParams(
                collective_id=0, has_side_effects=True, vmem_limit_bytes=56 * 1024 * 1024),
        )(now, prev, vel, eps, dlt, tilt, azim, aper)

    return jax.shard_map(
        local,
        mesh=mesh,
        in_specs=(
            P("shot", None, "gx", "gy", None),
            P("shot", None, "gx", "gy", None),
            P("gx", "gy", None),
            P("gx", "gy", None),
            P("gx", "gy", None),
            P("gx", "gy", None),
            P("gx", "gy", None),
            P("shot", "gx", "gy"),
        ),
        out_specs=(P("shot", None, "gx", "gy", None), P("gx", "gy", None)),
        check_vma=False,
    )
```

time: 223 us -> 58.3 us (0.26)
  other arithmetic: 88.9 us -> 0 us
  waiting for transfers between devices: 68.2 us -> 0 us
  Pallas kernels: 0 us -> 52.9 us
  starting transfers between devices: 45.1 us -> 0 us
  between operations: 15.3 us -> 1.3 us
    pallas_call x0 -> x1, Pallas kernels: none -> 52.9 us  [local(): pl.pallas_call(functools.partial(kernel, (ngx, X, Y, Z)), out_shape=(jax....]
    psum x1 -> x0, waiting for transfers between devices: 51.8 us -> none  [local(): image = lax.psum(covered * correlation, 'shot') / ITERS]
    ppermute x16 -> x0, starting transfers between devices: 45 us -> none  [the longest x8 28.8 us: extended(): lax.ppermute(lax.slice_in_dim(block, block.shape[dim] - width, None, axis...]
    sub x4 -> x0, other arithmetic: 44 us -> none  [advance(): across = second_x + second_y + second_z - along]
    concatenate x7 -> x0, other arithmetic: 22.4 us -> none  [extended(): block = jnp.concatenate([low, block, high], axis=dim)]
    ppermute x16 -> x0, waiting for transfers between devices: 16.4 us -> none  [the longest x8 16.3 us: extended(): lax.ppermute(lax.slice_in_dim(block, block.shape[dim] - width, None, axis...]
    another operation x8 -> x0, other arithmetic: 12.8 us -> none  [advance(): return jnp.stack([next_p, next_q], axis=2).reshape(centre.shape)]
    mul x2 -> x0, other arithmetic: 7.35 us -> none  [the longest x1 6.06 us: advance(): normal_x * normal_x * second_x + normal_y * normal_y * second_y]
  transfers between devices with their start and end apart: 17 -> 0, of which waited for: 9 -> 0; matrix products, arithmetic and copies ran while one was open for 3% -> 0% of each run, Pallas kernels for 0% -> 0%
where the time goes in v1:
time: 58.3 us; the launch traced here: 58.1 us
  Pallas kernels  52.9 us (91%)
  local copies, waits for them, and re-layouts  3.93 us (7%)
  between operations  1.3 us (2%)
    pallas_call x1, Pallas kernels, local(): pl.pallas_call(functools.partial(kernel, (ngx, X, Y, Z)), out_shape=(jax....  52.9 us
    unnamed x4, local copies, waits for them, and re-layouts  3.93 us

profile of v1, /device:TPU:7, one launch (start us, length us, event | category | flops | bytes accessed | tf_op | source)
XLA Modules:
  0.0 58.1 jit_solution(3761688506404917133)
XLA Ops:
  1.3 52.9 %shard_map.95 = (f32[1,4,32,32,128]{4,3,2,1,0:T(8,128)}, f32[32,32,128]{2,1,0:T(8,128)}) custom-call(f32[1,4,32,32,128]{4,3,2,1,0:T(8,128)} %now.1, f32[1,4,32,32,128]{4,3,2,1,0:T(8,128)} %prev.1, f32[32,32,128]{2,1,0:T(8,128)} %vel.1, f32[32,32,128]{2,1,0:T(8,128)} %eps.1, f32[32,32,128]{2,1,0:T(8,128)} %dlt.1, s32[32,32,128]{2,1,0:T(8,128)} %tilt.1, ...), custom_call_target="tpu_custom_call" | custom-call | tf_op jit(solution)/shard_map/pallas_call | solution.py:374
  54.2 0.0 copy-start
  54.2 3.1 %copy.13 = f32[1,4,32,32,128]{4,3,2,1,0:T(8,128)} copy(f32[1,4,32,32,128]{4,3,2,1,0:T(8,128)} %get-tuple-element.4) | data formatting | bytes 4194304
  57.3 0.0 copy-done
  57.3 0.8 %copy.14 = f32[32,32,128]{2,1,0:T(8,128)} copy(f32[32,32,128]{2,1,0:T(8,128)S(1)} %copy-done) | data formatting | bytes 1048576
Async XLA Ops:
  54.2 3.1 %copy-start = (f32[32,32,128]{2,1,0:T(8,128)S(1)}, f32[32,32,128]{2,1,0:T(8,128)}, u32[]{:S(2)}) copy-start(f32[32,32,128]{2,1,0:T(8,128)} %get-tuple-element.5) | copy-start | bytes 1572868

commit v2 on v1

--- a/solution.py
+++ b/solution.py
@@ -45,7 +45,7 @@
 
 
 def kernel(sizes, now, prev, vel, eps, dlt, tilt, azim, aper, wave_out, img_out,
-           U, M, A, K, corr, P_, Q, PC, QC, R1, R2, IMG, local, ssem, rsem, isem, osem):
+           U, M, A, K, corr, P_, Q, PC, QC, R1, R2, R3, local, ssem, rsem, isem):
     ngx, X, Y, Z = sizes
     T = Y // 8
     shot, gx, gy = lax.axis_index("shot"), lax.axis_index("gx"), lax.axis_index("gy")
@@ -149,24 +149,29 @@
     def send_y(t):
         par = t % 2
         for f in range(F):
-            P_[t, f] = U[par, f, pl.ds(1, X), y_send, :]
             PC[t, 0, pl.ds(f, 1), :] = U[par, f, 1, pl.ds(y_send, 1), :]
             PC[t, 1, pl.ds(f, 1), :] = U[par, f, X, pl.ds(y_send, 1), :]
+
+        @pl.when(has_l)
+        def _():
+            halo(t, 3).start()
+
+        @pl.when(has_r)
+        def _():
+            halo(t, 4).start()
+
+        for f in range(F):
+            P_[t, f] = U[par, f, pl.ds(1, X), y_send, :]
         halo(t, 2).start()
 
-        @pl.when(has_l)
-        def _():
-            halo(t, 3).start()
-
-        @pl.when(has_r)
-        def _():
-            halo(t, 4).start()
-
-    def receive(t):
+    def receive_y(t):
         par = t % 2
         halo(t, 2).wait_recv()
         for f in range(F):
             U[par, f, pl.ds(1, X), y_recv, :] = Q[t, f]
+
+    def receive_x(t):
+        par = t % 2
 
         @pl.when(has_r)
         def _():
@@ -205,9 +210,9 @@
     for i in range(1, 6):
         loads[i].wait()
 
-    def model(x, c):
-        for j in range(T):
-            rows = pl.ds(8 * j, 8)
+    def model(i, c):
+        for n in range(2 * T):
+            x, rows = 2 * i + n // T, pl.ds(8 * (n % T), 8)
             n_x, n_y, n_z = normals(A[0, x, rows, :], A[1, x, rows, :])
             v = M[0, x, rows, :]
             gain = 1.0 + 2.0 * M[1, x, rows, :]
@@ -225,143 +230,177 @@
             K[CV, x, rows, :] = v
         return c
 
-    lax.fori_loop(0, X, model, 0)
+    lax.fori_loop(0, X // 2, model, 0)
     loads[6].wait()
     covered = aper[0, 0, 0].astype(jnp.float32) * (1.0 / ITERS)
 
-    def segment(t, row, first, count, unroll):
+    edge_row = PAD + (Y - 8) * (1 - gy)
+    inner_row = PAD + 8 * gy
+
+    def group(t, x, row):
         a, b = t % 2, 1 - t % 2
         row = pl.multiple_of(row, 8)
-        yrow = pl.multiple_of(row - PAD, 8)
-
-        def plane(f, x):
-            mid = U[a, f, x, pl.ds(row, 8), :]
-            up, down = U[a, f, x, pl.ds(row + 1, 8), :], U[a, f, x, pl.ds(row - 1, 8), :]
-            return mid, up - down, up + down
-
-        def body(x, carry):
-            rows = pl.ds(yrow, 8)
-            k = [K[i, x - 1, rows, :] for i in range(NK)]
-            cxx, cyy = 1.0 - k[AXX], 1.0 - k[AYY]
-            cap, cam = mask_p - k[AP], mask_m - k[AM]
-            ahead, fresh, op = [], [], []
-            for f in range(F):
-                f0, e0, f1, e1, ys = carry[f]
-                f2, e2, ys2 = plane(f, x + 1)
-                ahead.append((f1, e1, f2, e2, ys2))
-                xs, dx, exy = f2 + f0, f2 - f0, e2 - e0
-                tp = k[BP] * dx + k[CP] * e1
-                tm = k[BM] * dx + k[CM] * e1
-                mix = k[BXY] * exy
-                if f % 2 == 0:
-                    sp, sm = cap * f1 - tp, cam * f1 + tm
-                    side = cxx * xs + cyy * ys - mix
-                else:
-                    sp, sm = k[AP] * f1 + tp, k[AM] * f1 - tm
-                    side = k[AXX] * xs + k[AYY] * ys + mix
-                op.append(side + (pltpu.roll(sp, Z - 1, 1) + pltpu.roll(sm, 1, 1)))
-            for pair in range(F // 2):
-                p, q = carry[2 * pair][2], carry[2 * pair + 1][2]
-                p2, q2 = p + p, q + q
-                across = op[2 * pair] - (p2 + p2)
-                along = op[2 * pair + 1] - q2
-                p_old = U[b, 2 * pair, x, pl.ds(row, 8), :]
-                q_old = U[b, 2 * pair + 1, x, pl.ds(row, 8), :]
-                p_new = (p2 - p_old) + (k[CG] * across + k[CR] * along)
-                q_new = (q2 - q_old) + (k[CR] * across + k[CV] * along)
-                U[b, 2 * pair, x, pl.ds(row, 8), :] = p_new
-                U[b, 2 * pair + 1, x, pl.ds(row, 8), :] = q_new
-                fresh.append(p_new)
-            prod = fresh[0] * fresh[1]
-            if t > 0:
-                prod = prod + corr[x - 1, rows, :]
+        here, rows = pl.ds(row, 8), pl.ds(pl.multiple_of(row - PAD, 8), 8)
+        k = [K[i, x - 1, rows, :] for i in range(NK)]
+        cxx, cyy = 1.0 - k[AXX], 1.0 - k[AYY]
+        cap, cam = mask_p - k[AP], mask_m - k[AM]
+        centre, op, fresh = [], [], []
+        for f in range(F):
+            def at(off_x, off_y):
+                return U[a, f, x + off_x, pl.ds(row + off_y, 8), :]
+
+            m0, m1, m2 = at(-1, 0), at(0, 0), at(1, 0)
+            up, down = at(0, 1), at(0, -1)
+            dy, ys = up - down, up + down
+            dx, xs = m2 - m0, m2 + m0
+            dxy = (at(1, 1) - at(1, -1)) - (at(-1, 1) - at(-1, -1))
+            tp = k[BP] * dx + k[CP] * dy
+            tm = k[BM] * dx + k[CM] * dy
+            mix = k[BXY] * dxy
+            if f % 2 == 0:
+                sp, sm = cap * m1 - tp, cam * m1 + tm
+                side = cxx * xs + cyy * ys - mix
+            else:
+                sp, sm = k[AP] * m1 + tp, k[AM] * m1 - tm
+                side = k[AXX] * xs + k[AYY] * ys + mix
+            op.append(side + (pltpu.roll(sp, Z - 1, 1) + pltpu.roll(sm, 1, 1)))
+            centre.append(m1)
+        for pair in range(F // 2):
+            fp, fq = 2 * pair, 2 * pair + 1
+            p, q = centre[fp], centre[fq]
+            p2, q2 = p + p, q + q
+            across, along = op[fp] - (p2 + p2), op[fq] - q2
+            p_new = (p2 - U[b, fp, x, here, :]) + (k[CG] * across + k[CR] * along)
+            q_new = (q2 - U[b, fq, x, here, :]) + (k[CR] * across + k[CV] * along)
             if t == ITERS - 1:
-                prod = prod * covered
-            corr[x - 1, rows, :] = prod
-            return tuple(ahead)
-
-        def start(f):
-            f0, e0, _ = plane(f, first - 1)
-            return (f0, e0) + plane(f, first)
-
-        carry = tuple(start(f) for f in range(F))
-
-        def several(i, carry):
-            for u in range(unroll):
-                carry = body(first + i * unroll + u, carry)
-            return carry
-
-        if count == unroll:
-            several(0, carry)
+                wave_out[0, fp, x - 1, rows, :] = p_new
+                wave_out[0, fq, x - 1, rows, :] = q_new
+            else:
+                U[b, fp, x, here, :] = p_new
+                U[b, fq, x, here, :] = q_new
+            fresh.append(p_new)
+        prod = fresh[0] * fresh[1]
+        if t > 0:
+            prod = prod + corr[x - 1, rows, :]
+        if t == ITERS - 1:
+            prod = prod * covered
+        corr[x - 1, rows, :] = prod
+
+    def interior(t):
+        def body(i, c):
+            for u in range(3):
+                for k in range(T - 1):
+                    group(t, 2 + 3 * i + u, inner_row + 8 * k)
+            return c
+
+        lax.fori_loop(0, (X - 2) // 3, body, 0)
+
+    def y_edge(t):
+        def body(i, c):
+            for u in range(10):
+                group(t, 2 + 10 * i + u, edge_row)
+            return c
+
+        lax.fori_loop(0, (X - 2) // 10, body, 0)
+
+    def x_edges(t):
+        for j in range(T):
+            group(t, 1, PAD + 8 * j)
+            group(t, X, PAD + 8 * j)
+
+    H = X // 2
+    in_rows = pl.ds(pl.multiple_of(8 * gy, 8), Y - 8)
+    ed_rows = pl.ds(pl.multiple_of((Y - 8) * (1 - gy), 8), 8)
+
+    def chunk(n, h):
+        if n == 0:
+            return pl.ds(1 + h * (H - 1), H - 1), in_rows
+        if n == 1:
+            return pl.ds(1 + h * (H - 1), H - 1), ed_rows
+        return pl.ds(h * (X - 1), 1), pl.ds(0, Y)
+
+    def image_copy(n, phase):
+        mine, theirs = chunk(n, core), chunk(n, 1 - core)
+
+        def make(src, dst, dev):
+            return pltpu.make_async_remote_copy(
+                src_ref=src, dst_ref=dst, send_sem=isem.at[0, phase, n], recv_sem=isem.at[1, phase, n],
+                device_id=dev, device_id_type=MESH)
+
+        if phase == 0:
+            return make(corr.at[theirs], R1.at[theirs], dev_c)
+        if phase == 1:
+            return make(R1.at[mine], R2.at[mine], dev_z)
+        return make(R3.at[mine], R3.at[mine], dev_c)
+
+    def over(n, h, fn):
+        xs, rows = chunk(n, h)
+
+        def body(i, c):
+            for j in range(rows.size // 8):
+                fn(xs.start + i, pl.ds(pl.multiple_of(rows.start + 8 * j, 8), 8))
+            return c
+
+        if xs.size == 1:
+            body(0, 0)
         else:
-            lax.fori_loop(0, count // unroll, several, carry)
-
-    edge_row = PAD + (Y - 8) * (1 - gy)
-    inner_row = PAD + 8 * gy
+            lax.fori_loop(0, xs.size, body, 0)
+
+    def image_chips(n):
+        image_copy(n, 0).wait_recv()
+
+        def add(x, rows):
+            R1[x, rows, :] = R1[x, rows, :] + corr[x, rows, :]
+
+        over(n, core, add)
+        image_copy(n, 1).start()
+
+    def image_gather(n):
+        image_copy(n, 1).wait_recv()
+
+        def add(x, rows):
+            total = R1[x, rows, :] + R2[x, rows, :]
+            R3[x, rows, :] = total
+            img_out[x, rows, :] = total
+
+        over(n, core, add)
+        image_copy(n, 2).start()
+
+    def image_finish(n):
+        image_copy(n, 2).wait_recv()
+
+        def put(x, rows):
+            img_out[x, rows, :] = R3[x, rows, :]
+
+        over(n, 1 - core, put)
+        for phase in range(3):
+            image_copy(n, phase).wait_send()
+
+    last = ITERS - 1
     for t in range(ITERS):
-        receive(t)
+        interior(t)
+        if t == last:
+            image_copy(0, 0).start()
+        receive_y(t)
         if t > 0:
             sent(t - 1)
-        segment(t, edge_row, 1, X, 2)
-
-        def ends(k, c, t=t):
-            segment(t, inner_row + 8 * k, 1, 1, 1)
-            segment(t, inner_row + 8 * k, X, 1, 1)
-            return c
-
-        lax.fori_loop(0, T - 1, ends, 0)
-        if t < ITERS - 1:
+        y_edge(t)
+        if t == last:
+            image_copy(1, 0).start()
+            image_chips(0)
+        receive_x(t)
+        x_edges(t)
+        if t < last:
             send_x(t + 1)
             send_y(t + 1)
-
-        def inner(k, c, t=t):
-            segment(t, inner_row + 8 * k, 2, X - 2, 2)
-            return c
-
-        lax.fori_loop(0, T - 1, inner, 0)
-    sent(ITERS - 1)
-
-    last = ITERS % 2
-    store = pltpu.make_async_copy(U.at[last, :, pl.ds(1, X), pl.ds(PAD, Y), :], wave_out.at[0], osem.at[0])
-    store.start()
-
-    H = X // 2
-    mine, theirs = pl.ds(core * H, H), pl.ds((1 - core) * H, H)
-
-    def image_copy(i, src, dst, dev):
-        return pltpu.make_async_remote_copy(
-            src_ref=src, dst_ref=dst, send_sem=isem.at[0, i], recv_sem=isem.at[1, i],
-            device_id=dev, device_id_type=MESH)
-
-    first = image_copy(0, corr.at[theirs], R1, dev_c)
-    first.start()
-    first.wait()
-
-    def add1(x, c):
-        for j in range(T):
-            rows = pl.ds(8 * j, 8)
-            R1[x, rows, :] = R1[x, rows, :] + corr[core * H + x, rows, :]
-        return c
-
-    lax.fori_loop(0, H, add1, 0)
-    second = image_copy(1, R1, R2, dev_z)
-    second.start()
-    second.wait()
-
-    def add2(x, c):
-        for j in range(T):
-            rows = pl.ds(8 * j, 8)
-            IMG[core * H + x, rows, :] = R1[x, rows, :] + R2[x, rows, :]
-        return c
-
-    lax.fori_loop(0, H, add2, 0)
-    third = image_copy(2, IMG.at[mine], IMG.at[mine], dev_c)
-    third.start()
-    third.wait()
-    out = pltpu.make_async_copy(IMG, img_out, osem.at[1])
-    out.start()
-    out.wait()
-    store.wait()
+    image_copy(2, 0).start()
+    image_chips(1)
+    image_chips(2)
+    for n in range(3):
+        image_gather(n)
+    for n in range(3):
+        image_finish(n)
+    sent(last)
 
 
 def solution(mesh):
@@ -369,13 +408,13 @@
 
     def local(now, prev, vel, eps, dlt, tilt, azim, aper):
         X, Y, Z = vel.shape
-        any_, vm = pl.BlockSpec(memory_space=pl.ANY), pltpu.VMEM
+        hbm, vm = pl.BlockSpec(memory_space=pltpu.HBM), pltpu.VMEM
         f32 = jnp.float32
         return pl.pallas_call(
             functools.partial(kernel, (ngx, X, Y, Z)),
             out_shape=(jax.ShapeDtypeStruct(now.shape, f32), jax.ShapeDtypeStruct(vel.shape, f32)),
-            in_specs=[any_] * 7 + [pl.BlockSpec(memory_space=pltpu.SMEM)],
-            out_specs=(any_, any_),
+            in_specs=[hbm] * 7 + [pl.BlockSpec(memory_space=pltpu.SMEM)],
+            out_specs=(pl.BlockSpec(memory_space=vm), pl.BlockSpec(memory_space=vm)),
             scratch_shapes=[
                 vm((2, F, X + 2, Y + 2 * PAD, Z), f32),
                 vm((3, X, Y, Z), f32),
@@ -386,17 +425,16 @@
                 vm((ITERS, F, X, Z), f32),
                 vm((ITERS, 2, F, Z), f32),
                 vm((ITERS, 2, F, Z), f32),
-                vm((X // 2, Y, Z), f32),
-                vm((X // 2, Y, Z), f32),
+                vm((X, Y, Z), f32),
+                vm((X, Y, Z), f32),
                 vm((X, Y, Z), f32),
                 pltpu.SemaphoreType.DMA((7,)),
                 pltpu.SemaphoreType.DMA((ITERS, 5)),
                 pltpu.SemaphoreType.DMA((ITERS, 5)),
-                pltpu.SemaphoreType.DMA((2, 3)),
-                pltpu.SemaphoreType.DMA((2,)),
+                pltpu.SemaphoreType.DMA((2, 3, 3)),
             ],
             compiler_params=pltpu.CompilerParams(
-                collective_id=0, has_side_effects=True, vmem_limit_bytes=56 * 1024 * 1024),
+                collective_id=0, has_side_effects=True, vmem_limit_bytes=58 * 1024 * 1024),
         )(now, prev, vel, eps, dlt, tilt, azim, aper)
 
     return jax.shard_map(

time: 58.3 us -> 43.2 us (0.74)
  Pallas kernels: 52.9 us -> 37.8 us
    pallas_call x1, Pallas kernels: 52.9 us -> 37.8 us  [local(): pl.pallas_call(functools.partial(kernel, (ngx, X, Y, Z)), out_shape=(jax....]
where the time goes in v2:
time: 43.2 us; the launch traced here: 43 us
  Pallas kernels  37.8 us (87%)
  local copies, waits for them, and re-layouts  3.93 us (9%)
  between operations  1.3 us (3%)
    pallas_call x1, Pallas kernels, local(): pl.pallas_call(functools.partial(kernel, (ngx, X, Y, Z)), out_shape=(jax....  37.8 us
    unnamed x4, local copies, waits for them, and re-layouts  3.93 us

profile of v2, /device:TPU:7, one launch (start us, length us, event | category | flops | bytes accessed | tf_op | source)
XLA Modules:
  0.0 43.0 jit_solution(17229923065669182576)
XLA Ops:
  1.3 37.8 %shard_map.95 = (f32[1,4,32,32,128]{4,3,2,1,0:T(8,128)}, f32[32,32,128]{2,1,0:T(8,128)}) custom-call(f32[1,4,32,32,128]{4,3,2,1,0:T(8,128)} %now.1, f32[1,4,32,32,128]{4,3,2,1,0:T(8,128)} %prev.1, f32[32,32,128]{2,1,0:T(8,128)} %vel.1, f32[32,32,128]{2,1,0:T(8,128)} %eps.1, f32[32,32,128]{2,1,0:T(8,128)} %dlt.1, s32[32,32,128]{2,1,0:T(8,128)} %tilt.1, ...), custom_call_target="tpu_custom_call" | custom-call | tf_op jit(solution)/shard_map/pallas_call | solution.py:413
  39.1 0.0 copy-start
  39.1 3.1 %copy.13 = f32[1,4,32,32,128]{4,3,2,1,0:T(8,128)} copy(f32[1,4,32,32,128]{4,3,2,1,0:T(8,128)} %get-tuple-element.4) | data formatting | bytes 4194304
  42.2 0.0 copy-done
  42.2 0.8 %copy.14 = f32[32,32,128]{2,1,0:T(8,128)} copy(f32[32,32,128]{2,1,0:T(8,128)S(1)} %copy-done) | data formatting | bytes 1048576
Async XLA Ops:
  39.1 3.1 %copy-start = (f32[32,32,128]{2,1,0:T(8,128)S(1)}, f32[32,32,128]{2,1,0:T(8,128)}, u32[]{:S(2)}) copy-start(f32[32,32,128]{2,1,0:T(8,128)} %get-tuple-element.5) | copy-start | bytes 1572868

commit v3 on v2

v3 whole, which is shorter than its diff:
```python
import functools
import math

import jax
import jax.numpy as jnp
from jax import lax
from jax.experimental import pallas as pl
from jax.experimental.pallas import tpu as pltpu
from jax.sharding import PartitionSpec as P

ITERS = 4
F = 4
PAD = 8
MESH = pl.DeviceIdType.MESH
NK = 12
AXX, AYY, BXY, AP, AM, BP, BM, CP, CM, CG, CR, CV = range(NK)


def sin_poly(x, x2):
    return x * (1.0 + x2 * (-1.0 / 6 + x2 * (1.0 / 120 + x2 * (-1.0 / 5040 + x2 * (1.0 / 362880 + x2 * (-1.0 / 39916800 + x2 * (1.0 / 6227020800)))))))


def cos_poly(x2):
    return 1.0 + x2 * (-0.5 + x2 * (1.0 / 24 + x2 * (-1.0 / 720 + x2 * (1.0 / 40320 + x2 * (-1.0 / 3628800 + x2 * (1.0 / 479001600 - x2 * (1.0 / 87178291200)))))))


def normals(tilt, azimuth):
    theta = tilt.astype(jnp.float32) * (math.pi / 180.0)
    t2 = theta * theta
    sin_t, cos_t = sin_poly(theta, t2), cos_poly(t2)
    h = (azimuth - 180).astype(jnp.float32) * (math.pi / 360.0)
    h2 = h * h
    s, c = sin_poly(h, h2), cos_poly(h2)
    s2 = s + s
    return sin_t * (s2 * s - 1.0), -(sin_t * (s2 * c)), cos_t


def kernel(sizes, now, prev, vel, eps, dlt, tilt, azim, aper, wave_out, img_out,
           U, M, A, K, corr, P_, Q, PC, QC, QY, R1, R2, R3, D, local, ssem, rsem, isem, dsem, osem):
    ngx, X, Y, Z = sizes
    T = Y // 8
    shot, gx, gy = lax.axis_index("shot"), lax.axis_index("gx"), lax.axis_index("gy")
    has_l, has_r = gx > 0, gx < ngx - 1
    core = lax.rem(shot, 2)
    core_pair = shot + 1 - 2 * core
    z_pair = lax.rem(shot + 2, 4)
    other = 1 - gy
    dev_y = (shot, gx, other)
    dev_c, dev_z = (core_pair, gx, gy), (z_pair, gx, gy)
    dev_zc = (lax.rem(core_pair + 2, 4), gx, gy)
    first_side = (lax.rem(gx, 4) == 0).astype(jnp.int32)
    sides = (first_side, 1 - first_side)

    def has(side):
        return jnp.logical_or(jnp.logical_and(side == 0, has_l), jnp.logical_and(side == 1, has_r))
    y_send = PAD + (Y - 1) * (1 - gy)
    y_recv = PAD - 1 + (Y + 1) * (1 - gy)

    loads = []
    for i, ref in enumerate((tilt, azim)):
        loads.append(pltpu.make_async_copy(ref, A.at[i], local.at[i]))
    for i, ref in enumerate((vel, eps, dlt)):
        loads.append(pltpu.make_async_copy(ref, M.at[i], local.at[2 + i]))
    for i, ref in enumerate((now, prev)):
        loads.append(pltpu.make_async_copy(ref.at[0], U.at[i, :, pl.ds(1, X), pl.ds(PAD, Y), :], local.at[5 + i]))
    for copy in loads:
        copy.start()

    barrier = pltpu.get_barrier_semaphore()

    def hello(dev):
        pl.semaphore_signal(barrier, inc=1, device_id=dev, device_id_type=MESH)

    for dev in (dev_y, dev_c, dev_z, dev_zc):
        hello(dev)

    @pl.when(has_l)
    def _():
        hello((shot, gx - 1, gy))
        hello((shot, gx - 1, other))

    @pl.when(has_r)
    def _():
        hello((shot, gx + 1, gy))
        hello((shot, gx + 1, other))

    zero_tile = jnp.zeros((8, Z), jnp.float32)

    def zero_rows(x, c):
        for par in range(2):
            for f in range(F):
                U[par, f, x, pl.ds(0, 8), :] = zero_tile
                U[par, f, x, pl.ds(PAD + Y, 8), :] = zero_tile
        return c

    lax.fori_loop(0, X + 2, zero_rows, 0)

    def zero_plane(x):
        for par in range(2):
            for f in range(F):
                for j in range(T):
                    U[par, f, x, pl.ds(PAD + 8 * j, 8), :] = zero_tile

    @pl.when(jnp.logical_not(has_l))
    def _():
        zero_plane(0)

    @pl.when(jnp.logical_not(has_r))
    def _():
        zero_plane(X + 1)

    pl.semaphore_wait(barrier, 4 + 2 * has_l.astype(jnp.int32) + 2 * has_r.astype(jnp.int32))

    def x_copy(t, side):
        plane = 1 + side * (X - 1)
        return pltpu.make_async_remote_copy(
            src_ref=now.at[0, :, plane - 1] if t == 0 else U.at[t % 2, :, plane, pl.ds(PAD, Y), :],
            dst_ref=U.at[t % 2, :, (1 - side) * (X + 1), pl.ds(PAD, Y), :],
            send_sem=ssem.at[t, side], recv_sem=rsem.at[t, 1 - side],
            device_id=(shot, gx + 2 * side - 1, gy), device_id_type=MESH)

    y_line = (Y - 1) * (1 - gy)

    def corner_copy(t, side):
        return pltpu.make_async_remote_copy(
            src_ref=now.at[0, :, side * (X - 1), y_line, :] if t == 0 else PC.at[t, side], dst_ref=QC.at[t, 1 - side],
            send_sem=ssem.at[t, 3 + side], recv_sem=rsem.at[t, 4 - side],
            device_id=(shot, gx + 2 * side - 1, other), device_id_type=MESH)

    def y_copy(t):
        return pltpu.make_async_remote_copy(
            src_ref=now.at[0, :, :, y_line, :] if t == 0 else P_.at[t], dst_ref=Q.at[t],
            send_sem=ssem.at[t, 2], recv_sem=rsem.at[t, 2], device_id=dev_y, device_id_type=MESH)

    def y_end_copy(t, side):
        return pltpu.make_async_remote_copy(
            src_ref=PC.at[t, side], dst_ref=QY.at[t, side], send_sem=ssem.at[t, 5 + side], recv_sem=rsem.at[t, 5 + side],
            device_id=dev_y, device_id_type=MESH)

    def send_x(t, side):
        @pl.when(has(side))
        def _():
            x_copy(t, side).start()

    def send_corner(t, side):
        if t > 0:
            for f in range(F):
                PC[t, side, pl.ds(f, 1), :] = U[t % 2, f, 1 + side * (X - 1), pl.ds(y_send, 1), :]
            y_end_copy(t, side).start()

        @pl.when(has(side))
        def _():
            corner_copy(t, side).start()

    def send_y(t):
        if t > 0:
            for f in range(F):
                P_[t, f] = U[t % 2, f, pl.ds(1, X), y_send, :]
        y_copy(t).start()

    def receive_y(t):
        y_copy(t).wait_recv()
        for f in range(F):
            U[t % 2, f, pl.ds(1, X), y_recv, :] = Q[t, f]
        if t > 0:
            for side in range(2):
                y_end_copy(t, side).wait_recv()
                for f in range(F):
                    U[t % 2, f, 1 + side * (X - 1), pl.ds(y_recv, 1), :] = QY[t, side, pl.ds(f, 1), :]

    def receive_x(t, side):
        @pl.when(has(side))
        def _():
            x_copy(t, 1 - side).wait_recv()
            corner_copy(t, 1 - side).wait_recv()
            for f in range(F):
                U[t % 2, f, side * (X + 1), pl.ds(y_recv, 1), :] = QC[t, side, pl.ds(f, 1), :]

    def sent(t, side):
        @pl.when(has(side))
        def _():
            x_copy(t, side).wait_send()
            corner_copy(t, side).wait_send()

    send_y(0)
    for side in sides:
        send_x(0, side)
        send_corner(0, side)

    lane = lax.broadcasted_iota(jnp.int32, (8, Z), 1)
    mask_p = jnp.where(lane == 0, 0.0, 1.0)
    mask_m = jnp.where(lane == Z - 1, 0.0, 1.0)
    for i in range(5):
        loads[i].wait()

    def model(i, c):
        for n in range(4 * T):
            x, rows = 4 * i + n // T, pl.ds(8 * (n % T), 8)
            n_x, n_y, n_z = normals(A[0, x, rows, :], A[1, x, rows, :])
            v = M[0, x, rows, :]
            gain = 1.0 + 2.0 * M[1, x, rows, :]
            root = jnp.sqrt(1.0 + 2.0 * M[2, x, rows, :])
            half = 0.5 * n_z
            zz, xz, yz = n_z * n_z, half * n_x, half * n_y
            K[AXX, x, rows, :] = n_x * n_x
            K[AYY, x, rows, :] = n_y * n_y
            K[BXY, x, rows, :] = 0.5 * n_x * n_y
            for value, plus, minus in ((zz, AP, AM), (xz, BP, BM), (yz, CP, CM)):
                K[plus, x, rows, :] = pltpu.roll(value, 1, 1) * mask_p
                K[minus, x, rows, :] = pltpu.roll(value, Z - 1, 1) * mask_m
            K[CG, x, rows, :] = v * gain
            K[CR, x, rows, :] = v * root
            K[CV, x, rows, :] = v
        return c

    lax.fori_loop(0, X // 4, model, 0)
    loads[5].wait()
    loads[6].wait()
    covered = aper[0, 0, 0].astype(jnp.float32) * (1.0 / ITERS)

    edge_row = PAD + (Y - 8) * (1 - gy)
    inner_row = PAD + 8 * gy

    def group(t, x, row, edge=None):
        a, b = t % 2, 1 - t % 2
        row = pl.multiple_of(row, 8)
        here, rows = pl.ds(row, 8), pl.ds(pl.multiple_of(row - PAD, 8), 8)
        k = [K[i, x - 1, rows, :] for i in range(NK)]
        cxx, cyy = 1.0 - k[AXX], 1.0 - k[AYY]
        cap, cam = mask_p - k[AP], mask_m - k[AM]
        centre, op, fresh = [], [], []
        for f in range(F):
            def at(off_x, off_y):
                return U[a, f, x + off_x, pl.ds(row + off_y, 8), :]

            m0, m1, m2 = at(-1, 0), at(0, 0), at(1, 0)
            up, down = at(0, 1), at(0, -1)
            dy, ys = up - down, up + down
            dx, xs = m2 - m0, m2 + m0
            dxy = (at(1, 1) - at(1, -1)) - (at(-1, 1) - at(-1, -1))
            tp = k[BP] * dx + k[CP] * dy
            tm = k[BM] * dx + k[CM] * dy
            mix = k[BXY] * dxy
            if f % 2 == 0:
                sp, sm = cap * m1 - tp, cam * m1 + tm
                side = cxx * xs + cyy * ys - mix
            else:
                sp, sm = k[AP] * m1 + tp, k[AM] * m1 - tm
                side = k[AXX] * xs + k[AYY] * ys + mix
            op.append(side + (pltpu.roll(sp, Z - 1, 1) + pltpu.roll(sm, 1, 1)))
            centre.append(m1)
        for pair in range(F // 2):
            fp, fq = 2 * pair, 2 * pair + 1
            p, q = centre[fp], centre[fq]
            p2, q2 = p + p, q + q
            across, along = op[fp] - (p2 + p2), op[fq] - q2
            p_new = (p2 - U[b, fp, x, here, :]) + (k[CG] * across + k[CR] * along)
            q_new = (q2 - U[b, fq, x, here, :]) + (k[CR] * across + k[CV] * along)
            U[b, fp, x, here, :] = p_new
            U[b, fq, x, here, :] = q_new
            fresh.append(p_new)
        prod = fresh[0] * fresh[1]
        if t > 0:
            prod = prod + corr[x - 1, rows, :]
        if t == ITERS - 1:
            prod = prod * covered
        if t == ITERS - 1 and edge is not None:
            D[shot, edge, rows, :] = prod
        else:
            corr[x - 1, rows, :] = prod

    far_row = PAD + 16 * gy
    near_row = PAD + Y - 16 - (Y - 24) * gy

    def interior(t):
        def body(i, c):
            for u in range(3):
                for k in range(T - 1):
                    group(t, 2 + 3 * i + u, inner_row + 8 * k)
            return c

        lax.fori_loop(0, (X - 2) // 3, body, 0)

    def core_part(t):
        def body(i, c):
            for u in range(4):
                for k in range(T - 2):
                    group(t, 3 + 4 * i + u, far_row + 8 * k)
            return c

        lax.fori_loop(0, (X - 4) // 4, body, 0)

    def rest_part(t):
        for x in (2, X - 1):
            for k in range(T - 2):
                group(t, x, far_row + 8 * k)

        def body(i, c):
            for u in range(10):
                group(t, 2 + 10 * i + u, near_row)
            return c

        lax.fori_loop(0, (X - 2) // 10, body, 0)

    def y_edge(t):
        def body(i, c):
            for u in range(10):
                group(t, 2 + 10 * i + u, edge_row)
            return c

        lax.fori_loop(0, (X - 2) // 10, body, 0)

    def x_edge(t, side):
        for j in range(T):
            group(t, 1 + side * (X - 1), PAD + 8 * j, side)

    far = pl.ds(pl.multiple_of(16 * gy, 8), 8 * (T - 2))
    near = pl.ds(pl.multiple_of(Y - 16 - (Y - 24) * gy, 8), 8)
    edge_rows = pl.ds(pl.multiple_of((Y - 8) * (1 - gy), 8), 8)
    CHUNKS = ((2, (X - 4) // 2, (X - 4) // 2, far), (1, X // 2 - 1, X // 2 - 1, near), (1, X // 2 - 1, X // 2 - 1, edge_rows), (1, X - 3, 1, far))
    NC = len(CHUNKS)

    def chunk(n, h):
        low, hop, count, rows = CHUNKS[n]
        return pl.ds(low + h * hop, count), rows

    def image_copy(n, phase):
        mine, theirs = chunk(n, core), chunk(n, 1 - core)

        def make(src, dst, dev):
            return pltpu.make_async_remote_copy(
                src_ref=src, dst_ref=dst, send_sem=isem.at[0, phase, n], recv_sem=isem.at[1, phase, n],
                device_id=dev, device_id_type=MESH)

        if phase == 0:
            return make(corr.at[theirs], R1.at[theirs], dev_c)
        if phase == 1:
            return make(R1.at[mine], R2.at[mine], dev_z)
        return make(R3.at[mine], R3.at[mine], dev_c)

    def over(n, h, fn):
        xs, rows = chunk(n, h)

        def body(i, c):
            for j in range(rows.size // 8):
                fn(xs.start + i, pl.ds(pl.multiple_of(rows.start + 8 * j, 8), 8))
            return c

        if xs.size == 1:
            body(0, 0)
        else:
            lax.fori_loop(0, xs.size, body, 0)

    def image_chips(n):
        image_copy(n, 0).wait_recv()

        def add(x, rows):
            R1[x, rows, :] = R1[x, rows, :] + corr[x, rows, :]

        over(n, core, add)
        image_copy(n, 1).start()

    def image_gather(n):
        image_copy(n, 1).wait_recv()

        def add(x, rows):
            R3[x, rows, :] = R1[x, rows, :] + R2[x, rows, :]

        over(n, core, add)
        image_copy(n, 2).start()

    def out_copy(n, h):
        xs, rows = chunk(n, h)
        return pltpu.make_async_copy(R3.at[xs, rows, :], img_out.at[xs, rows, :], osem.at[n, h])

    def image_finish(n):
        out_copy(n, core).start()
        image_copy(n, 2).wait_recv()
        out_copy(n, 1 - core).start()

    def edge_out(side):
        plane = side * (X - 1)
        return pltpu.make_async_copy(R3.at[plane], img_out.at[plane], osem.at[4, side])

    peers = (dev_c, dev_z, dev_zc)

    def direct(i, side, slot):
        return pltpu.make_async_remote_copy(
            src_ref=D.at[slot, side], dst_ref=D.at[slot, side], send_sem=dsem.at[0, i, side], recv_sem=dsem.at[1, slot, side],
            device_id=peers[i], device_id_type=MESH)

    last = ITERS - 1
    for t in range(ITERS):
        if t == 1:
            interior(0)
        if t == last:
            image_chips(0)
            rest_part(t)
            image_copy(1, 0).start()
            image_copy(3, 0).start()
            image_chips(1)
            image_chips(3)
        elif t > 0:
            interior(t)
        if t == last - 1:
            core_part(last)
            image_copy(0, 0).start()
        receive_y(t)
        y_edge(t)
        if t < last:
            send_y(t + 1)
        else:
            image_copy(2, 0).start()
        for side in sides:
            receive_x(t, side)
            if t > 0:
                sent(t - 1, side)
            x_edge(t, side)
            if t < last:
                send_x(t + 1, side)
                send_corner(t + 1, side)
            else:
                for i in (1, 2, 0):
                    direct(i, side, shot).start()
    image_chips(2)
    wave_copy = pltpu.make_async_copy(U.at[ITERS % 2, :, pl.ds(1, X), pl.ds(PAD, Y), :], wave_out.at[0], osem.at[5, 0])
    wave_copy.start()
    for n in (0, 1, 3):
        image_gather(n)
    for n in (0, 1, 3):
        image_finish(n)
    image_gather(2)
    for side in sides:
        for i, slot in enumerate((core_pair, z_pair, lax.rem(core_pair + 2, 4))):
            direct(i, side, slot).wait_recv()
        for j in range(T):
            rows = pl.ds(8 * j, 8)
            total = (D[0, side, rows, :] + D[1, side, rows, :]) + (D[2, side, rows, :] + D[3, side, rows, :])
            R3[side * (X - 1), rows, :] = total
        edge_out(side).start()
    image_finish(2)
    for n in range(NC):
        for phase in range(3):
            image_copy(n, phase).wait_send()
    for side in sides:
        sent(last, side)
        for i in range(3):
            direct(i, side, shot).wait_send()
        for t in range(1, ITERS):
            y_end_copy(t, side).wait_send()
    for t in range(ITERS):
        y_copy(t).wait_send()
    for n in range(NC):
        for h in range(2):
            out_copy(n, h).wait()
    for side in sides:
        edge_out(side).wait()
    wave_copy.wait()


def hand_over(wave, image, wave_out, image_out, wave_buf, image_buf, sem):
    parts = [(wave.at[0, f, pl.ds(h * 16, 16)], wave_buf.at[f, pl.ds(h * 16, 16)], wave_out.at[0, f, pl.ds(h * 16, 16)]) for f in range(F) for h in range(2)]
    parts.append((image, image_buf, image_out))
    reads = [pltpu.make_async_copy(src, buf, sem.at[0, n]) for n, (src, buf, _) in enumerate(parts)]
    writes = [pltpu.make_async_copy(buf, dst, sem.at[1, n]) for n, (_, buf, dst) in enumerate(parts)]
    for copy in reads:
        copy.start()
    for read, write in zip(reads, writes):
        read.wait()
        write.start()
    for copy in writes:
        copy.wait()


def solution(mesh):
    ngx = mesh.shape["gx"]

    def local(now, prev, vel, eps, dlt, tilt, azim, aper):
        X, Y, Z = vel.shape
        hbm, vm = pl.BlockSpec(memory_space=pltpu.HBM), pltpu.VMEM
        f32 = jnp.float32
        wave, image = pl.pallas_call(
            functools.partial(kernel, (ngx, X, Y, Z)),
            out_shape=(jax.ShapeDtypeStruct(now.shape, f32), jax.ShapeDtypeStruct(vel.shape, f32)),
            in_specs=[hbm] * 7 + [pl.BlockSpec(memory_space=pltpu.SMEM)],
            out_specs=(hbm, hbm),
            scratch_shapes=[
                vm((2, F, X + 2, Y + 2 * PAD, Z), f32),
                vm((3, X, Y, Z), f32),
                vm((2, X, Y, Z), jnp.int32),
                vm((NK, X, Y, Z), f32),
                vm((X, Y, Z), f32),
                vm((ITERS, F, X, Z), f32),
                vm((ITERS, F, X, Z), f32),
                vm((ITERS, 2, F, Z), f32),
                vm((ITERS, 2, F, Z), f32),
                vm((ITERS, 2, F, Z), f32),
                vm((X, Y, Z), f32),
                vm((X, Y, Z), f32),
                vm((X, Y, Z), f32),
                vm((4, 2, Y, Z), f32),
                pltpu.SemaphoreType.DMA((7,)),
                pltpu.SemaphoreType.DMA((ITERS, 7)),
                pltpu.SemaphoreType.DMA((ITERS, 7)),
                pltpu.SemaphoreType.DMA((2, 3, 4)),
                pltpu.SemaphoreType.DMA((2, 4, 2)),
                pltpu.SemaphoreType.DMA((6, 2)),
            ],
            compiler_params=pltpu.CompilerParams(
                collective_id=0, has_side_effects=True, vmem_limit_bytes=58 * 1024 * 1024),
        )(now, prev, vel, eps, dlt, tilt, azim, aper)
        return pl.pallas_call(
            hand_over,
            out_shape=(jax.ShapeDtypeStruct(now.shape, f32), jax.ShapeDtypeStruct(vel.shape, f32)),
            in_specs=[hbm] * 2,
            out_specs=(hbm, hbm),
            scratch_shapes=[vm(now.shape[1:], f32), vm(vel.shape, f32), pltpu.SemaphoreType.DMA((2, 2 * F + 1))],
            compiler_params=pltpu.CompilerParams(vmem_limit_bytes=58 * 1024 * 1024),
        )(wave, image)

    return jax.shard_map(
        local,
        mesh=mesh,
        in_specs=(
            P("shot", None, "gx", "gy", None),
            P("shot", None, "gx", "gy", None),
            P("gx", "gy", None),
            P("gx", "gy", None),
            P("gx", "gy", None),
            P("gx", "gy", None),
            P("gx", "gy", None),
            P("shot", "gx", "gy"),
        ),
        out_specs=(P("shot", None, "gx", "gy", None), P("gx", "gy", None)),
        check_vma=False,
    )
```

time: 43.2 us -> 38.7 us (0.90)
  local copies, waits for them, and re-layouts: 3.93 us -> 0 us
  Pallas kernels: 37.8 us -> 37.3 us
    unnamed x4 -> x0, local copies, waits for them, and re-layouts: 3.93 us -> none
    pallas_call x1, Pallas kernels: 37.8 us -> 34.6 us  [local(): pl.pallas_call(functools.partial(kernel, (ngx, X, Y, Z)), out_shape=(jax....]
    pallas_call x0 -> x1, Pallas kernels: none -> 2.63 us  [local(): pl.pallas_call(hand_over, out_shape=(jax.ShapeDtypeStruct(now.shape, f32)...]
where the time goes in v3:
time: 38.7 us; the launch traced here: 38.6 us
  Pallas kernels  37.3 us (96%)
  between operations  1.29 us (3%)
    pallas_call x1, Pallas kernels, local(): pl.pallas_call(functools.partial(kernel, (ngx, X, Y, Z)), out_shape=(jax....  34.6 us
    pallas_call x1, Pallas kernels, local(): pl.pallas_call(hand_over, out_shape=(jax.ShapeDtypeStruct(now.shape, f32)...  2.63 us

profile of v3, /device:TPU:7, one launch (start us, length us, event | category | flops | bytes accessed | tf_op | source)
XLA Modules:
  0.0 38.6 jit_solution(8950468457233250953)
XLA Ops:
  1.3 34.6 %shard_map.95 = (f32[1,4,32,32,128]{4,3,2,1,0:T(8,128)}, f32[32,32,128]{2,1,0:T(8,128)}) custom-call(f32[1,4,32,32,128]{4,3,2,1,0:T(8,128)} %now.1, f32[1,4,32,32,128]{4,3,2,1,0:T(8,128)} %prev.1, f32[32,32,128]{2,1,0:T(8,128)} %vel.1, f32[32,32,128]{2,1,0:T(8,128)} %eps.1, f32[32,32,128]{2,1,0:T(8,128)} %dlt.1, s32[32,32,128]{2,1,0:T(8,128)} %tilt.1, ...), custom_call_target="tpu_custom_call" | custom-call | tf_op jit(solution)/shard_map/pallas_call | solution.py:482
  35.9 2.6 %shard_map.96 = (f32[1,4,32,32,128]{4,3,2,1,0:T(8,128)}, f32[32,32,128]{2,1,0:T(8,128)}) custom-call(f32[1,4,32,32,128]{4,3,2,1,0:T(8,128)} %get-tuple-element.4.wave, f32[32,32,128]{2,1,0:T(8,128)} %get-tuple-element.5.image), custom_call_target="tpu_custom_call" | custom-call | tf_op jit(solution)/shard_map/pallas_call | solution.py:512

commit v4 on v3

--- a/solution.py
+++ b/solution.py
@@ -36,7 +36,7 @@
 
 
 def kernel(sizes, now, prev, vel, eps, dlt, tilt, azim, aper, wave_out, img_out,
-           U, M, A, K, corr, P_, Q, PC, QC, QY, R1, R2, R3, D, local, ssem, rsem, isem, dsem, osem):
+           U, M, A, K, corr, early, P_, Q, PC, QC, QY, R1, R2, R3, D, line, local, ssem, rsem, isem, dsem, osem):
     ngx, X, Y, Z = sizes
     T = Y // 8
     shot, gx, gy = lax.axis_index("shot"), lax.axis_index("gx"), lax.axis_index("gy")
@@ -172,6 +172,10 @@
         @pl.when(has(side))
         def _():
             x_copy(t, 1 - side).wait_recv()
+
+    def receive_corner(t, side):
+        @pl.when(has(side))
+        def _():
             corner_copy(t, 1 - side).wait_recv()
             for f in range(F):
                 U[t % 2, f, side * (X + 1), pl.ds(y_recv, 1), :] = QC[t, side, pl.ds(f, 1), :]
@@ -184,8 +188,8 @@
 
     send_y(0)
     for side in sides:
+        send_corner(0, side)
         send_x(0, side)
-        send_corner(0, side)
 
     lane = lax.broadcasted_iota(jnp.int32, (8, Z), 1)
     mask_p = jnp.where(lane == 0, 0.0, 1.0)
@@ -221,7 +225,7 @@
     edge_row = PAD + (Y - 8) * (1 - gy)
     inner_row = PAD + 8 * gy
 
-    def group(t, x, row, edge=None):
+    def group(t, x, row, edge=None, ahead=False):
         a, b = t % 2, 1 - t % 2
         row = pl.multiple_of(row, 8)
         here, rows = pl.ds(row, 8), pl.ds(pl.multiple_of(row - PAD, 8), 8)
@@ -256,8 +260,9 @@
             across, along = op[fp] - (p2 + p2), op[fq] - q2
             p_new = (p2 - U[b, fp, x, here, :]) + (k[CG] * across + k[CR] * along)
             q_new = (q2 - U[b, fq, x, here, :]) + (k[CR] * across + k[CV] * along)
-            U[b, fp, x, here, :] = p_new
-            U[b, fq, x, here, :] = q_new
+            if not ahead:
+                U[b, fp, x, here, :] = p_new
+                U[b, fq, x, here, :] = q_new
             fresh.append(p_new)
         prod = fresh[0] * fresh[1]
         if t > 0:
@@ -266,6 +271,8 @@
             prod = prod * covered
         if t == ITERS - 1 and edge is not None:
             D[shot, edge, rows, :] = prod
+        elif ahead:
+            early[x - 1] = prod
         else:
             corr[x - 1, rows, :] = prod
 
@@ -302,17 +309,20 @@
 
         lax.fori_loop(0, (X - 2) // 10, body, 0)
 
-    def y_edge(t):
+    def y_edge(t, ahead=False):
         def body(i, c):
             for u in range(10):
-                group(t, 2 + 10 * i + u, edge_row)
+                group(t, 2 + 10 * i + u, edge_row, ahead=ahead)
             return c
 
         lax.fori_loop(0, (X - 2) // 10, body, 0)
 
     def x_edge(t, side):
-        for j in range(T):
-            group(t, 1 + side * (X - 1), PAD + 8 * j, side)
+        plane = 1 + side * (X - 1)
+        for k in range(T - 1):
+            group(t, plane, inner_row + 8 * k, side)
+        receive_corner(t, side)
+        group(t, plane, edge_row, side)
 
     far = pl.ds(pl.multiple_of(16 * gy, 8), 8 * (T - 2))
     near = pl.ds(pl.multiple_of(Y - 16 - (Y - 24) * gy, 8), 8)
@@ -333,7 +343,7 @@
                 device_id=dev, device_id_type=MESH)
 
         if phase == 0:
-            return make(corr.at[theirs], R1.at[theirs], dev_c)
+            return make(early.at[theirs[0]] if n == 2 else corr.at[theirs], R1.at[theirs], dev_c)
         if phase == 1:
             return make(R1.at[mine], R2.at[mine], dev_z)
         return make(R3.at[mine], R3.at[mine], dev_c)
@@ -355,7 +365,7 @@
         image_copy(n, 0).wait_recv()
 
         def add(x, rows):
-            R1[x, rows, :] = R1[x, rows, :] + corr[x, rows, :]
+            R1[x, rows, :] = R1[x, rows, :] + (early[x] if n == 2 else corr[x, rows, :])
 
         over(n, core, add)
         image_copy(n, 1).start()
@@ -374,9 +384,11 @@
         return pltpu.make_async_copy(R3.at[xs, rows, :], img_out.at[xs, rows, :], osem.at[n, h])
 
     def image_finish(n):
-        out_copy(n, core).start()
+        if n != 2:
+            out_copy(n, core).start()
         image_copy(n, 2).wait_recv()
-        out_copy(n, 1 - core).start()
+        if n != 2:
+            out_copy(n, 1 - core).start()
 
     def edge_out(side):
         plane = side * (X - 1)
@@ -385,6 +397,10 @@
     peers = (dev_c, dev_z, dev_zc)
 
     def direct(i, side, slot):
+        if side is None:
+            return pltpu.make_async_remote_copy(
+                src_ref=line.at[slot], dst_ref=line.at[slot], send_sem=dsem.at[0, i, 2], recv_sem=dsem.at[1, slot, 2],
+                device_id=peers[i], device_id_type=MESH)
         return pltpu.make_async_remote_copy(
             src_ref=D.at[slot, side], dst_ref=D.at[slot, side], send_sem=dsem.at[0, i, side], recv_sem=dsem.at[1, slot, side],
             device_id=peers[i], device_id_type=MESH)
@@ -398,8 +414,11 @@
             rest_part(t)
             image_copy(1, 0).start()
             image_copy(3, 0).start()
+            y_edge(t, ahead=True)
+            image_copy(2, 0).start()
             image_chips(1)
             image_chips(3)
+            image_chips(2)
         elif t > 0:
             interior(t)
         if t == last - 1:
@@ -410,44 +429,50 @@
         if t < last:
             send_y(t + 1)
         else:
-            image_copy(2, 0).start()
+            line[shot] = corr[:, y_line, :]
+            for i in (1, 2, 0):
+                direct(i, None, shot).start()
         for side in sides:
             receive_x(t, side)
             if t > 0:
                 sent(t - 1, side)
             x_edge(t, side)
             if t < last:
+                send_corner(t + 1, side)
                 send_x(t + 1, side)
-                send_corner(t + 1, side)
             else:
                 for i in (1, 2, 0):
                     direct(i, side, shot).start()
-    image_chips(2)
     wave_copy = pltpu.make_async_copy(U.at[ITERS % 2, :, pl.ds(1, X), pl.ds(PAD, Y), :], wave_out.at[0], osem.at[5, 0])
     wave_copy.start()
-    for n in (0, 1, 3):
+    order = (0, 1, 3, 2)
+    for n in order:
         image_gather(n)
-    for n in (0, 1, 3):
+    for n in order:
         image_finish(n)
-    image_gather(2)
+        for phase in range(3):
+            image_copy(n, phase).wait_send()
+    slots = (core_pair, z_pair, lax.rem(core_pair + 2, 4))
+    for i, slot in enumerate(slots):
+        direct(i, None, slot).wait_recv()
+    R3[:, y_line, :] = (line[0] + line[1]) + (line[2] + line[3])
+    for h in range(2):
+        out_copy(2, h).start()
     for side in sides:
-        for i, slot in enumerate((core_pair, z_pair, lax.rem(core_pair + 2, 4))):
+        for i, slot in enumerate(slots):
             direct(i, side, slot).wait_recv()
         for j in range(T):
             rows = pl.ds(8 * j, 8)
             total = (D[0, side, rows, :] + D[1, side, rows, :]) + (D[2, side, rows, :] + D[3, side, rows, :])
             R3[side * (X - 1), rows, :] = total
         edge_out(side).start()
-    image_finish(2)
-    for n in range(NC):
-        for phase in range(3):
-            image_copy(n, phase).wait_send()
     for side in sides:
         sent(last, side)
+        for t in range(1, ITERS):
+            y_end_copy(t, side).wait_send()
+    for side in (*sides, None):
         for i in range(3):
             direct(i, side, shot).wait_send()
-        for t in range(1, ITERS):
-            y_end_copy(t, side).wait_send()
     for t in range(ITERS):
         y_copy(t).wait_send()
     for n in range(NC):
@@ -459,7 +484,12 @@
 
 
 def hand_over(wave, image, wave_out, image_out, wave_buf, image_buf, sem):
-    parts = [(wave.at[0, f, pl.ds(h * 16, 16)], wave_buf.at[f, pl.ds(h * 16, 16)], wave_out.at[0, f, pl.ds(h * 16, 16)]) for f in range(F) for h in range(2)]
+    half = wave.shape[2] // 2
+    parts = []
+    for f in range(F):
+        for h in range(2):
+            xs = pl.ds(h * half, half)
+            parts.append((wave.at[0, f, xs], wave_buf.at[f, xs], wave_out.at[0, f, xs]))
     parts.append((image, image_buf, image_out))
     reads = [pltpu.make_async_copy(src, buf, sem.at[0, n]) for n, (src, buf, _) in enumerate(parts)]
     writes = [pltpu.make_async_copy(buf, dst, sem.at[1, n]) for n, (_, buf, dst) in enumerate(parts)]
@@ -490,6 +520,7 @@
                 vm((2, X, Y, Z), jnp.int32),
                 vm((NK, X, Y, Z), f32),
                 vm((X, Y, Z), f32),
+                vm((X, 8, Z), f32),
                 vm((ITERS, F, X, Z), f32),
                 vm((ITERS, F, X, Z), f32),
                 vm((ITERS, 2, F, Z), f32),
@@ -499,11 +530,12 @@
                 vm((X, Y, Z), f32),
                 vm((X, Y, Z), f32),
                 vm((4, 2, Y, Z), f32),
+                vm((4, X, Z), f32),
                 pltpu.SemaphoreType.DMA((7,)),
                 pltpu.SemaphoreType.DMA((ITERS, 7)),
                 pltpu.SemaphoreType.DMA((ITERS, 7)),
                 pltpu.SemaphoreType.DMA((2, 3, 4)),
-                pltpu.SemaphoreType.DMA((2, 4, 2)),
+                pltpu.SemaphoreType.DMA((2, 4, 3)),
                 pltpu.SemaphoreType.DMA((6, 2)),
             ],
             compiler_params=pltpu.CompilerParams(

time: 38.7 us -> 37.2 us (0.961)
  Pallas kernels: 37.3 us -> 35.7 us
    pallas_call x1, Pallas kernels: 34.6 us -> 33.1 us  [local(): pl.pallas_call(functools.partial(kernel, (ngx, X, Y, Z)), out_shape=(jax....]
where the time goes in v4:
time: 37.2 us; the launch traced here: 37 us
  Pallas kernels  35.7 us (96%)
  between operations  1.29 us (3%)
    pallas_call x1, Pallas kernels, local(): pl.pallas_call(functools.partial(kernel, (ngx, X, Y, Z)), out_shape=(jax....  33.1 us
    pallas_call x1, Pallas kernels, local(): pl.pallas_call(hand_over, out_shape=(jax.ShapeDtypeStruct(now.shape, f32)...  2.63 us

profile of v4, /device:TPU:7, one launch (start us, length us, event | category | flops | bytes accessed | tf_op | source)
XLA Modules:
  0.0 37.0 jit_solution(649856333396404727)
XLA Ops:
  1.3 33.1 %shard_map.95 = (f32[1,4,32,32,128]{4,3,2,1,0:T(8,128)}, f32[32,32,128]{2,1,0:T(8,128)}) custom-call(f32[1,4,32,32,128]{4,3,2,1,0:T(8,128)} %now.1, f32[1,4,32,32,128]{4,3,2,1,0:T(8,128)} %prev.1, f32[32,32,128]{2,1,0:T(8,128)} %vel.1, f32[32,32,128]{2,1,0:T(8,128)} %eps.1, f32[32,32,128]{2,1,0:T(8,128)} %dlt.1, s32[32,32,128]{2,1,0:T(8,128)} %tilt.1, ...), custom_call_target="tpu_custom_call" | custom-call | tf_op jit(solution)/shard_map/pallas_call | solution.py:512
  34.4 2.6 %shard_map.96 = (f32[1,4,32,32,128]{4,3,2,1,0:T(8,128)}, f32[32,32,128]{2,1,0:T(8,128)}) custom-call(f32[1,4,32,32,128]{4,3,2,1,0:T(8,128)} %get-tuple-element.4.wave, f32[32,32,128]{2,1,0:T(8,128)} %get-tuple-element.5.image), custom_call_target="tpu_custom_call" | custom-call | tf_op jit(solution)/shard_map/pallas_call | solution.py:544

commit v5 on v4

--- a/solution.py
+++ b/solution.py
@@ -319,10 +319,9 @@
 
     def x_edge(t, side):
         plane = 1 + side * (X - 1)
-        for k in range(T - 1):
-            group(t, plane, inner_row + 8 * k, side)
         receive_corner(t, side)
-        group(t, plane, edge_row, side)
+        for j in range(T):
+            group(t, plane, PAD + 8 * j, side)
 
     far = pl.ds(pl.multiple_of(16 * gy, 8), 8 * (T - 2))
     near = pl.ds(pl.multiple_of(Y - 16 - (Y - 24) * gy, 8), 8)

time: 37.2 us -> 37.1 us (level)
  no operation moved by 1% of the time
where the time goes in v5:
time: 37.1 us; the launch traced here: 36.9 us
  Pallas kernels  35.6 us (96%)
  between operations  1.29 us (3%)
    pallas_call x1, Pallas kernels, local(): pl.pallas_call(functools.partial(kernel, (ngx, X, Y, Z)), out_shape=(jax....  33 us
    pallas_call x1, Pallas kernels, local(): pl.pallas_call(hand_over, out_shape=(jax.ShapeDtypeStruct(now.shape, f32)...  2.63 us

profile of v5, /device:TPU:7, one launch (start us, length us, event | category | flops | bytes accessed | tf_op | source)
XLA Modules:
  0.0 36.9 jit_solution(9802318462786777055)
XLA Ops:
  1.3 33.0 %shard_map.95 = (f32[1,4,32,32,128]{4,3,2,1,0:T(8,128)}, f32[32,32,128]{2,1,0:T(8,128)}) custom-call(f32[1,4,32,32,128]{4,3,2,1,0:T(8,128)} %now.1, f32[1,4,32,32,128]{4,3,2,1,0:T(8,128)} %prev.1, f32[32,32,128]{2,1,0:T(8,128)} %vel.1, f32[32,32,128]{2,1,0:T(8,128)} %eps.1, f32[32,32,128]{2,1,0:T(8,128)} %dlt.1, s32[32,32,128]{2,1,0:T(8,128)} %tilt.1, ...), custom_call_target="tpu_custom_call" | custom-call | tf_op jit(solution)/shard_map/pallas_call | solution.py:511
  34.3 2.6 %shard_map.96 = (f32[1,4,32,32,128]{4,3,2,1,0:T(8,128)}, f32[32,32,128]{2,1,0:T(8,128)}) custom-call(f32[1,4,32,32,128]{4,3,2,1,0:T(8,128)} %get-tuple-element.4.wave, f32[32,32,128]{2,1,0:T(8,128)} %get-tuple-element.5.image), custom_call_target="tpu_custom_call" | custom-call | tf_op jit(solution)/shard_map/pallas_call | solution.py:543

commit v6 on v5

--- a/solution.py
+++ b/solution.py
@@ -146,7 +146,6 @@
         if t > 0:
             for f in range(F):
                 PC[t, side, pl.ds(f, 1), :] = U[t % 2, f, 1 + side * (X - 1), pl.ds(y_send, 1), :]
-            y_end_copy(t, side).start()
 
         @pl.when(has(side))
         def _():
@@ -439,6 +438,7 @@
             if t < last:
                 send_corner(t + 1, side)
                 send_x(t + 1, side)
+                y_end_copy(t + 1, side).start()
             else:
                 for i in (1, 2, 0):
                     direct(i, side, shot).start()
@@ -483,12 +483,9 @@
 
 
 def hand_over(wave, image, wave_out, image_out, wave_buf, image_buf, sem):
-    half = wave.shape[2] // 2
     parts = []
     for f in range(F):
-        for h in range(2):
-            xs = pl.ds(h * half, half)
-            parts.append((wave.at[0, f, xs], wave_buf.at[f, xs], wave_out.at[0, f, xs]))
+        parts.append((wave.at[0, f], wave_buf.at[f], wave_out.at[0, f]))
     parts.append((image, image_buf, image_out))
     reads = [pltpu.make_async_copy(src, buf, sem.at[0, n]) for n, (src, buf, _) in enumerate(parts)]
     writes = [pltpu.make_async_copy(buf, dst, sem.at[1, n]) for n, (_, buf, dst) in enumerate(parts)]
@@ -545,7 +542,7 @@
             out_shape=(jax.ShapeDtypeStruct(now.shape, f32), jax.ShapeDtypeStruct(vel.shape, f32)),
             in_specs=[hbm] * 2,
             out_specs=(hbm, hbm),
-            scratch_shapes=[vm(now.shape[1:], f32), vm(vel.shape, f32), pltpu.SemaphoreType.DMA((2, 2 * F + 1))],
+            scratch_shapes=[vm(now.shape[1:], f32), vm(vel.shape, f32), pltpu.SemaphoreType.DMA((2, F + 1))],
             compiler_params=pltpu.CompilerParams(vmem_limit_bytes=58 * 1024 * 1024),
         )(wave, image)
 

time: 37.1 us -> 37 us (level)
  no operation moved by 1% of the time
where the time goes in v6:
time: 37 us; the launch traced here: 36.9 us
  Pallas kernels  35.6 us (96%)
  between operations  1.29 us (3%)
    pallas_call x1, Pallas kernels, local(): pl.pallas_call(functools.partial(kernel, (ngx, X, Y, Z)), out_shape=(jax....  33 us
    pallas_call x1, Pallas kernels, local(): pl.pallas_call(hand_over, out_shape=(jax.ShapeDtypeStruct(now.shape, f32)...  2.61 us

profile of v6, /device:TPU:7, one launch (start us, length us, event | category | flops | bytes accessed | tf_op | source)
XLA Modules:
  0.0 36.9 jit_solution(13327637279545194033)
XLA Ops:
  1.3 33.0 %shard_map.95 = (f32[1,4,32,32,128]{4,3,2,1,0:T(8,128)}, f32[32,32,128]{2,1,0:T(8,128)}) custom-call(f32[1,4,32,32,128]{4,3,2,1,0:T(8,128)} %now.1, f32[1,4,32,32,128]{4,3,2,1,0:T(8,128)} %prev.1, f32[32,32,128]{2,1,0:T(8,128)} %vel.1, f32[32,32,128]{2,1,0:T(8,128)} %eps.1, f32[32,32,128]{2,1,0:T(8,128)} %dlt.1, s32[32,32,128]{2,1,0:T(8,128)} %tilt.1, ...), custom_call_target="tpu_custom_call" | custom-call | tf_op jit(solution)/shard_map/pallas_call | solution.py:508
  34.3 2.6 %shard_map.96 = (f32[1,4,32,32,128]{4,3,2,1,0:T(8,128)}, f32[32,32,128]{2,1,0:T(8,128)}) custom-call(f32[1,4,32,32,128]{4,3,2,1,0:T(8,128)} %get-tuple-element.4.wave, f32[32,32,128]{2,1,0:T(8,128)} %get-tuple-element.5.image), custom_call_target="tpu_custom_call" | custom-call | tf_op jit(solution)/shard_map/pallas_call | solution.py:540
